TPU v7x, 256 devices: a whole 4x4x8 slice. The times are simulated.
256 devices in a mesh: dp: 32 (over x_hi, z, core), mp: 8 (over x_lo, y).
Axes of the slice: x: 4 (x_hi: 2, x_lo: 2; x = x_hi * 2 + x_lo), y: 4, z: 8, core: 2. Of those that a mesh axis runs over, the one named last changes fastest.
Arguments:
- context: bfloat16 [8192, 6144], P('dp', 'mp'), may hold values from -6 to 6
- out_grad: bfloat16 [8192, 6144], P('dp', 'mp'), may hold values from -1.0546875 to 1.0546875
- master: float32 [8, 36864, 128], P('mp', 'dp'), may hold values from -0.078125 to 0.078125
- moment_one: float32 [8, 36864, 128], P('mp', 'dp'), may hold values from -3 to 3
- moment_two: float32 [8, 36864, 128], P('mp', 'dp'), may hold values from 1 to 64
- new_owner: int32 [32], replicated, may hold values from 0 to 31, as said below
- old_pieces: int32 [32, 32, 36], replicated, may hold values from 0 to 36863, as said below
Outputs:
- proj_out: bfloat16 [8192, 6144], P('dp', 'mp')
- master_out: float32 [8, 36864, 128], P('mp', 'dp')
- moment_one_out: float32 [8, 36864, 128], P('mp', 'dp')
- moment_two_out: float32 [8, 36864, 128], P('mp', 'dp')
Inputs may be any that keep to these rules, and one draw needn't show every extreme that they name: `new_owner`: each index of dp appears exactly once. Every block number appears exactly once; old_pieces[i, j, :] lie from new_owner[j] * 1152 to new_owner[j] * 1152 + 1151.
All inputs are finite; a program needn't handle non-finite values.
Results may differ from a plain program's by a relative error of at most 0.015.
Values may be sent and summed in bfloat16 or wider, within the bound.
No kernel may reach another device: no remote copies, remote signals or barrier semaphores. Data moves between devices by JAX's collectives and lax.ppermute only.
A program may use at most 64 MiB of HBM per device.

v0:
```python
import jax
import jax.numpy as jnp
from jax import lax
from jax.sharding import PartitionSpec as P

beta_one = 0.9
beta_two = 0.999
learn_rate = 0.001
decay_rate = 0.1
epsilon = 1e-08
step_count = 100.0


def adamw(weights, first_moment, second_moment, gradient):
    first_new = beta_one * first_moment + (1.0 - beta_one) * gradient
    second_new = beta_two * second_moment + (1.0 - beta_two) * gradient * gradient
    corrected_first = first_new / (1.0 - beta_one**step_count)
    corrected_second = second_new / (1.0 - beta_two**step_count)
    update = corrected_first / (jnp.sqrt(corrected_second) + epsilon)
    weights_new = weights - learn_rate * (update + decay_rate * weights)
    return (weights_new, first_new, second_new)


def local(context, out_grad, master, moment_one, moment_two, new_owner, old_pieces):
    dp_count = lax.axis_size("dp")
    dp_index = lax.axis_index("dp")
    blocks = master.shape[1]
    block_width = master.shape[2]
    pieces = blocks // dp_count
    full_width = out_grad.shape[1] * lax.axis_size("mp")
    per_row = full_width // block_width
    slab_rows = blocks // per_row
    group_rows = context.shape[1]
    own_slab = new_owner[dp_index]
    sources = lax.dynamic_index_in_dim(old_pieces, dp_index, 1, keepdims=False)
    positions = (sources - own_slab * blocks).reshape(-1)

    def outgoing(state_array):
        return state_array.reshape(dp_count, pieces, block_width)

    def arrange(received):
        placed = (
            jnp.zeros((blocks, block_width), jnp.float32)
            .at[positions]
            .set(received.reshape(blocks, block_width))
        )
        return placed.reshape(slab_rows, full_width)

    row_order = jnp.arange(group_rows, dtype=jnp.int32)
    actual = new_owner[row_order // slab_rows] * slab_rows + row_order % slab_rows
    permuted = jnp.take(context, actual, axis=1)
    received = (
        lax.all_to_all(outgoing(master), "dp", split_axis=0, concat_axis=0, tiled=True),
        lax.all_to_all(outgoing(moment_one), "dp", split_axis=0, concat_axis=0, tiled=True),
        lax.all_to_all(outgoing(moment_two), "dp", split_axis=0, concat_axis=0, tiled=True),
    )
    weights = arrange(received[0])
    first_moment = arrange(received[1])
    second_moment = arrange(received[2])
    gathered = lax.all_gather(weights.astype(jnp.bfloat16), "dp", axis=0, tiled=True)
    partial_out = jnp.dot(permuted, gathered, preferred_element_type=jnp.float32)
    proj_out = lax.psum_scatter(partial_out, "mp", scatter_dimension=1, tiled=True).astype(
        jnp.bfloat16
    )
    cotangent = lax.all_gather(out_grad, "mp", axis=1, tiled=True)
    gradient = lax.psum_scatter(
        jnp.einsum("tr,td->rd", permuted, cotangent, preferred_element_type=jnp.float32).astype(
            jnp.bfloat16
        ),
        "dp",
        scatter_dimension=0,
        tiled=True,
    ).astype(jnp.float32)
    weights_new, first_new, second_new = adamw(weights, first_moment, second_moment, gradient)
    out_shape = (1, blocks, block_width)
    return (
        proj_out,
        weights_new.reshape(out_shape),
        first_new.reshape(out_shape),
        second_new.reshape(out_shape),
    )


def solution(mesh):
    placed = (
        P("dp", "mp"),
        P("dp", "mp"),
        P("mp", "dp", None),
        P("mp", "dp", None),
        P("mp", "dp", None),
        P(),
        P(),
    )
    return jax.shard_map(
        local,
        mesh=mesh,
        in_specs=placed,
        out_specs=(P("dp", "mp"), P("mp", "dp", None), P("mp", "dp", None), P("mp", "dp", None)),
        check_vma=False,
    )
```

profile of v0, /device:TPU:1, one launch (start us, length us, event | category | flops | bytes accessed | tf_op | source)
XLA Modules:
  0.0 428.6 jit_solution(6142448214314012248)
XLA Ops:
  7.9 1.2 copy.12
  10.0 1.9 fusion.22
  11.9 4.3 %fusion.15 = s32[768]{0:T(1024)S(1)} fusion(s32[]{:T(128)} %bitcast.25, s32[]{:T(128)} %bitcast.26, s32[]{:T(128)} %bitcast.27, s32[]{:T(128)} %bitcast.28, s32[]{:T(128)} %bitcast.29, s32[]{:T(128)} %bitcast.31, s32[]{:T(128)} %bitcast.30), kind=kLoop, calls=%fused_computation.72 | loop fusion | flops 17664 | bytes 3100 | tf_op jit(solution)/shard_map/gather | solution.py:50
  16.2 2.1 fusion.21
  18.3 15.7 %compare_and_fusion = (pred[768]{0:T(1024)(128)(4,1)S(1)}, s32[768]{0:T(1024)S(1)}) fusion(pred[768]{0:T(1024)(128)(4,1)S(1)} %compare_reduce_fusion, pred[768]{0:T(1024)(128)(4,1)S(1)} %compare_reduce_fusion.1, pred[768]{0:T(1024)(128)(4,1)S(1)} %compare_reduce_fusion.2, pred[768]{0:T(1024)(128)(4,1)S(1)} %compare_reduce_fusion.3, ...), kind=kLoop, calls=%fused_computation.70 | loop fusion | flops 29952 | bytes 26212 | tf_op jit(solution)/shard_map/jit(_take)/and | solution.py:51
  34.1 2.7 gather_fusion
  36.8 21.0 %all-gather.5.cloned.1.call-done = bf16[256,6144]{1,0:T(8,128)(2,1)} async-done(((bf16[256,768]{1,0:T(8,128)(2,1)}), bf16[256,6144]{1,0:T(8,128)(2,1)}) %all-gather.5.cloned.1.call-update) | async-done | bytes 3145744 | tf_op jit(solution)/shard_map/all_gather | solution.py:65
  57.7 7.2 %convolution_convert_fusion = bf16[768,6144]{1,0:T(8,128)(2,1)} fusion(bf16[256,6144]{1,0:T(8,128)(2,1)} %all-gather.5.cloned.1.call-done, bf16[768,256]{1,0:T(8,128)(2,1)S(1)} %gather_fusion, pred[768]{0:T(1024)(128)(4,1)S(1)} %get-tuple-element.7), kind=kOutput, calls=%fused_computation.4 | convolution fusion | flops 2420834304 | bytes 12976896 | tf_op jit(solution)/shard_map/tr,td->rd/dot_general | solution.py:67
  65.9 12.3 %all-to-all-start = ((f32[32,36,128]{2,1,0:T(8,128)}), f32[32,36,128]{2,1,0:T(8,128)S(1)}, u32[]{:S(2)}, u32[]{:S(2)}) async-start(f32[32,36,128]{2,1,0:T(8,128)} %reshape.152), calls=%async_computation | async-start | bytes 1310720 | tf_op jit(solution)/shard_map/all_to_all | solution.py:53
  79.1 19.6 %all-to-all-done = f32[32,36,128]{2,1,0:T(8,128)S(1)} async-done(((f32[32,36,128]{2,1,0:T(8,128)}), f32[32,36,128]{2,1,0:T(8,128)S(1)}, u32[]{:S(2)}, u32[]{:S(2)}) %all-to-all-start) | async-done | bytes 589856 | tf_op jit(solution)/shard_map/all_to_all | solution.py:53
  98.7 5.6 %all-to-all-start.1 = ((f32[32,36,128]{2,1,0:T(8,128)}), f32[32,36,128]{2,1,0:T(8,128)S(1)}, u32[]{:S(2)}, u32[]{:S(2)}) async-start(f32[32,36,128]{2,1,0:T(8,128)} %reshape.155), calls=%async_computation.2 | async-start | bytes 1310720 | tf_op jit(solution)/shard_map/all_to_all | solution.py:54
  105.2 19.7 %all-to-all-done.1 = f32[32,36,128]{2,1,0:T(8,128)S(1)} async-done(((f32[32,36,128]{2,1,0:T(8,128)}), f32[32,36,128]{2,1,0:T(8,128)S(1)}, u32[]{:S(2)}, u32[]{:S(2)}) %all-to-all-start.1) | async-done | bytes 589856 | tf_op jit(solution)/shard_map/all_to_all | solution.py:54
  124.9 5.6 %all-to-all-start.2 = ((f32[32,36,128]{2,1,0:T(8,128)}), f32[32,36,128]{2,1,0:T(8,128)S(1)}, u32[]{:S(2)}, u32[]{:S(2)}) async-start(f32[32,36,128]{2,1,0:T(8,128)} %reshape.157), calls=%async_computation.4 | async-start | bytes 1310720 | tf_op jit(solution)/shard_map/all_to_all | solution.py:55
  131.1 1.0 subtract_reduce_fusion
  132.3 6.2 %scatter_custom_fusion = f32[1152,128]{1,0:T(8,128)S(1)} fusion(s32[1152]{0:T(1024)S(1)} %fusion.9, f32[1152,128]{1,0:T(8,128)S(1)} %reshape.213, f32[]{:T(128)} %constant.38.clone.1), kind=kCustom, calls=%fused_computation.17 | custom fusion | bytes 589828 | tf_op jit(solution)/shard_map/scatter | solution.py:45
  139.4 6.7 %scatter_custom_fusion.1 = f32[1152,128]{1,0:T(8,128)S(1)} fusion(s32[1152]{0:T(1024)S(1)} %fusion.9, f32[1152,128]{1,0:T(8,128)} %reshape.221, f32[]{:T(128)} %constant.38.clone.1), kind=kCustom, calls=%fused_computation.15 | custom fusion | bytes 590336 | tf_op jit(solution)/shard_map/scatter | solution.py:45
  147.1 6.8 %all-to-all-done.2 = f32[32,36,128]{2,1,0:T(8,128)S(1)} async-done(((f32[32,36,128]{2,1,0:T(8,128)}), f32[32,36,128]{2,1,0:T(8,128)S(1)}, u32[]{:S(2)}, u32[]{:S(2)}) %all-to-all-start.2) | async-done | bytes 589856 | tf_op jit(solution)/shard_map/all_to_all | solution.py:55
  154.0 6.2 %scatter_custom_fusion.2 = f32[1152,128]{1,0:T(8,128)S(1)} fusion(s32[1152]{0:T(1024)S(1)} %fusion.9, f32[1152,128]{1,0:T(8,128)S(1)} %reshape.229, f32[]{:T(128)} %constant.38.clone.1), kind=kCustom, calls=%fused_computation.13 | custom fusion | bytes 589828 | tf_op jit(solution)/shard_map/scatter | solution.py:45
  161.1 67.5 %reduce-scatter.5.cloned.1.call-done = bf16[24,6144]{1,0:T(8,128)(2,1)} async-done(((bf16[768,6144]{1,0:T(8,128)(2,1)}), bf16[24,6144]{1,0:T(8,128)(2,1)}) %reduce-scatter.5.cloned.1.call-update) | async-done | bytes 294928 | tf_op jit(solution)/shard_map/reduce_scatter | solution.py:66
  228.7 2.5 multiply_subtract_fusion
  231.2 108.5 %all-gather.3.cloned.1.call-done = bf16[768,6144]{1,0:T(8,128)(2,1)} async-done(((bf16[24,6144]{1,0:T(8,128)(2,1)}), bf16[768,6144]{1,0:T(8,128)(2,1)}) %all-gather.3.cloned.1.call-update) | async-done | bytes 9437200 | tf_op jit(solution)/shard_map/all_gather | solution.py:60
  339.7 8.5 %fusion.8 = f32[256,6144]{1,0:T(8,128)} fusion(bf16[768,6144]{1,0:T(8,128)(2,1)} %all-gather.3.cloned.1.call-done, bf16[768,256]{1,0:T(8,128)(2,1)S(1)} %gather_fusion, pred[768]{0:T(1024)(128)(4,1)S(1)} %get-tuple-element.7), kind=kOutput, calls=%fused_computation.19 | convolution fusion | flops 2416115712 | bytes 16122624 | tf_op jit(solution)/shard_map/dot_general | solution.py:61
  350.9 69.3 %reduce-scatter.3.cloned.1.call-done = f32[256,768]{1,0:T(8,128)} async-done(((f32[256,6144]{1,0:T(8,128)}), f32[256,768]{1,0:T(8,128)}) %reduce-scatter.3.cloned.1.call-update) | async-done | bytes 786448 | tf_op jit(solution)/shard_map/reduce_scatter | solution.py:62
  420.2 1.9 convert_element_type.13
  (57 shorter events, 10.3 us)
Async XLA Ops:
  7.2 50.6 %all-gather.5.cloned.1.call-start = ((), (), s32[]{:S(2)}) async-start(), calls=%async_computation.7 | async-start | bytes 3538944 | tf_op jit(solution)/shard_map/all_gather | solution.py:65
  7.9 220.8 %reduce-scatter.5.cloned.1.call-start = ((), (), s32[]{:S(2)}) async-start(), calls=%async_computation.8 | async-start | bytes 9732096 | tf_op jit(solution)/shard_map/reduce_scatter | solution.py:66
  57.7 7.3 %copy-start = (f32[1,1152,128]{2,1,0:T(8,128)S(1)}, f32[1,1152,128]{2,1,0:T(8,128)}, u32[]{:S(2)}) copy-start(f32[1,1152,128]{2,1,0:T(8,128)} %param.9) | copy-start | bytes 1769476
  57.7 20.5 %copy-start.1 = (f32[1,1152,128]{2,1,0:T(8,128)S(1)}, f32[1,1152,128]{2,1,0:T(8,128)}, u32[]{:S(2)}) copy-start(f32[1,1152,128]{2,1,0:T(8,128)} %param.10) | copy-start | bytes 1769476
  65.0 39.3 %copy-start.2 = (f32[1,1152,128]{2,1,0:T(8,128)S(1)}, f32[1,1152,128]{2,1,0:T(8,128)}, u32[]{:S(2)}) copy-start(f32[1,1152,128]{2,1,0:T(8,128)} %param.11) | copy-start | bytes 1769476
  65.9 32.8 %all-to-all-start = ((f32[32,36,128]{2,1,0:T(8,128)}), f32[32,36,128]{2,1,0:T(8,128)S(1)}, u32[]{:S(2)}, u32[]{:S(2)}) async-start(f32[32,36,128]{2,1,0:T(8,128)} %reshape.152), calls=%async_computation | async-start | bytes 1310720 | tf_op jit(solution)/shard_map/all_to_all | solution.py:53
  98.7 26.2 %all-to-all-start.1 = ((f32[32,36,128]{2,1,0:T(8,128)}), f32[32,36,128]{2,1,0:T(8,128)S(1)}, u32[]{:S(2)}, u32[]{:S(2)}) async-start(f32[32,36,128]{2,1,0:T(8,128)} %reshape.155), calls=%async_computation.2 | async-start | bytes 1310720 | tf_op jit(solution)/shard_map/all_to_all | solution.py:54
  124.9 29.0 %all-to-all-start.2 = ((f32[32,36,128]{2,1,0:T(8,128)}), f32[32,36,128]{2,1,0:T(8,128)S(1)}, u32[]{:S(2)}, u32[]{:S(2)}) async-start(f32[32,36,128]{2,1,0:T(8,128)} %reshape.157), calls=%async_computation.4 | async-start | bytes 1310720 | tf_op jit(solution)/shard_map/all_to_all | solution.py:55
  130.5 209.2 %all-gather.3.cloned.1.call-start = ((), (), s32[]{:S(2)}) async-start(), calls=%async_computation.5 | async-start | bytes 9732096 | tf_op jit(solution)/shard_map/all_gather | solution.py:60
  231.2 189.0 %reduce-scatter.3.cloned.1.call-start = ((), (), s32[]{:S(2)}) async-start(), calls=%async_computation.6 | async-start | bytes 7077888 | tf_op jit(solution)/shard_map/reduce_scatter | solution.py:62
Sparse Core Ops, SparseCore 0:
  9.8 47.9 all-gather.4
  65.1 163.5 reduce-scatter.4
  232.0 107.6 all-gather.2
  348.3 71.8 reduce-scatter.2
where the time goes:
time: 430 us; the launch traced here: 429 us
  waiting for transfers between devices  313 us (73%)
  local copies, waits for them, and re-layouts  35.2 us (8%)
  other arithmetic  26.5 us (6%)
  starting transfers between devices  23.7 us (6%)
  matrix products  15.7 us (4%)
  between operations  14.6 us (3%)
    all_gather x1, waiting for transfers between devices, local(): lax.all_gather(weights.astype(jnp.bfloat16), 'dp', axis=0, tiled=True)  108 us
    reduce_scatter x1, waiting for transfers between devices, local(): lax.psum_scatter(partial_out, 'mp', scatter_dimension=1, tiled=True)  69.3 us
    reduce_scatter x1, waiting for transfers between devices, local(): lax.psum_scatter(jnp.einsum('tr,td->rd', permuted, cotangent, preferred_e...  67.5 us
    all_gather x1, waiting for transfers between devices, local(): cotangent = lax.all_gather(out_grad, 'mp', axis=1, tiled=True)  21 us
    all_to_all x1, waiting for transfers between devices, local(): lax.all_to_all(outgoing(moment_one), 'dp', split_axis=0, concat_axis=0, t...  19.7 us
    all_to_all x1, waiting for transfers between devices, local(): lax.all_to_all(outgoing(master), 'dp', split_axis=0, concat_axis=0, tiled...  19.6 us
    scatter x3, local copies, waits for them, and re-layouts, arrange(): placed = jnp.zeros((blocks, block_width), jnp.float32).at[positions].set(...  19 us
    and x1, other arithmetic, local(): permuted = jnp.take(context, actual, axis=1)  15.7 us
  transfers between devices with their start and end apart: 7, of which 7 were waited for; matrix products, arithmetic and copies ran while one was open for 13% of the time, Pallas kernels for 0%

commit v1 on v0

v1 whole, which is shorter than its diff:
```python
import jax
import jax.numpy as jnp
from jax import lax
from jax.sharding import Mesh, PartitionSpec as P

beta_one = 0.9
beta_two = 0.999
learn_rate = 0.001
decay_rate = 0.1
epsilon = 1e-08
step_count = 100.0

DP = ("xh", "z", "c")
MP = ("xl", "y")
DL = ("xh", "c")


def adamw(weights, first_moment, second_moment, gradient):
    first_new = beta_one * first_moment + (1.0 - beta_one) * gradient
    second_new = beta_two * second_moment + (1.0 - beta_two) * gradient * gradient
    corrected_first = first_new / (1.0 - beta_one**step_count)
    corrected_second = second_new / (1.0 - beta_two**step_count)
    update = corrected_first / (jnp.sqrt(corrected_second) + epsilon)
    weights_new = weights - learn_rate * (update + decay_rate * weights)
    return (weights_new, first_new, second_new)


def one_hot(index, count):
    rows = lax.broadcasted_iota(jnp.int32, (count, index.shape[0]), 0)
    return (rows == index[None, :]).astype(jnp.bfloat16)


def local(context, out_grad, master, moment_one, moment_two, new_owner, old_pieces):
    f32, bf16 = jnp.float32, jnp.bfloat16
    n_dp, n_mp = lax.axis_size(DP), lax.axis_size(MP)
    n_z, n_dl = lax.axis_size("z"), lax.axis_size(DL)
    n_xh, n_c = lax.axis_size("xh"), lax.axis_size("c")
    d = lax.axis_index(DP)
    blocks, width = master.shape[1:]
    tokens, cols = context.shape
    per_dev = cols // width
    per_row = per_dev * n_mp
    rows = blocks // per_row
    own_slab = new_owner[d]
    positions = (lax.dynamic_index_in_dim(old_pieces, d, 1, keepdims=False) - own_slab * blocks).reshape(-1)

    w_in = lax.all_to_all(master[0].astype(bf16), DP, 0, 0, tiled=True)
    moments = jnp.concatenate([moment_one[0], moment_two[0]], axis=1).astype(bf16)
    m_in = lax.all_to_all(moments, DP, 0, 0, tiled=True)

    owner_order = new_owner.reshape(n_xh, n_z, n_c).transpose(0, 2, 1).reshape(-1)
    wanted = (owner_order[:, None] * rows + jnp.arange(rows, dtype=jnp.int32)[None]).reshape(-1)
    columns = lax.broadcasted_iota(jnp.int32, (cols, cols), 1)
    select = (columns == wanted[:, None]).astype(bf16)
    ct = lax.dot_general(select, context, (((1,), (1,)), ((), ())), preferred_element_type=f32).astype(bf16)
    ct = lax.all_to_all(ct.reshape(n_dl, n_z * rows, tokens), DL, 0, 0, tiled=True)
    ct = lax.all_gather(ct, MP, axis=0, tiled=False)
    ct = ct.reshape(n_mp, n_dl, n_z, rows, tokens).transpose(0, 2, 3, 1, 4).reshape(n_mp * n_z * rows, n_dl * tokens)
    og = lax.all_gather(out_grad, DL, axis=0, tiled=True)

    grad = jnp.dot(ct, og, preferred_element_type=f32).astype(bf16)
    grad = lax.psum_scatter(grad.reshape(n_mp, n_z, rows, cols), "z", scatter_dimension=1, tiled=True)
    grad = lax.all_to_all(grad.reshape(n_mp, rows, cols), MP, 0, 0, tiled=True)
    grad = grad.reshape(n_mp, rows, per_dev, width).transpose(1, 0, 2, 3).reshape(blocks, width).astype(f32)

    w_at = (positions % per_row) * rows + positions // per_row
    w_t = jnp.dot(one_hot(w_at, blocks), w_in, preferred_element_type=f32).astype(bf16)
    w_t = lax.all_to_all(w_t.reshape(n_mp, per_dev, rows, width), MP, 0, 0, tiled=True)
    w_t = lax.all_gather(w_t, "z", axis=0, tiled=False)
    w_t = w_t.transpose(1, 0, 3, 2, 4).reshape(n_mp * n_z * rows, cols)
    out = lax.dot_general(ct, w_t, (((0,), (0,)), ((), ())), preferred_element_type=f32).astype(bf16)
    proj_out = lax.psum_scatter(out, DL, scatter_dimension=0, tiled=True)

    placed = jnp.dot(
        one_hot(positions, blocks), jnp.concatenate([w_in, m_in], axis=1), preferred_element_type=f32
    )
    weights, first_moment, second_moment = (placed[:, i * width : (i + 1) * width] for i in range(3))
    weights_new, first_new, second_new = adamw(weights, first_moment, second_moment, grad)
    return (proj_out, weights_new[None], first_new[None], second_new[None])


def solution(mesh):
    fine = Mesh(mesh.devices.reshape(2, 8, 2, 2, 4), DP[:2] + ("c",) + MP)
    placed = (P(DP, MP), P(DP, MP), P(MP, DP, None), P(MP, DP, None), P(MP, DP, None), P(), P())
    return jax.shard_map(
        local,
        mesh=fine,
        in_specs=placed,
        out_specs=(P(DP, MP), P(MP, DP, None), P(MP, DP, None), P(MP, DP, None)),
        check_vma=False,
    )
```

time: 430 us -> 252 us (0.59)
  waiting for transfers between devices: 313 us -> 121 us
  blocking collectives: 0 us -> 70.1 us
  local copies, waits for them, and re-layouts: 35.2 us -> 13.5 us
  other arithmetic: 26.5 us -> 6.02 us
  starting transfers between devices: 23.7 us -> 14 us
    reduce_scatter x2, waiting for transfers between devices: 137 us -> 41 us  [the longest x1 31.3 us: local(): proj_out = lax.psum_scatter(out, DL, scatter_dimension=0, tiled=True)]
    all_to_all x0 -> x3, blocking collectives: none -> 70.1 us  [the longest x1 39.4 us: local(): m_in = lax.all_to_all(moments, DP, 0, 0, tiled=True)]
    all_gather x2 -> x3, waiting for transfers between devices: 129 us -> 63.5 us  [the longest x1 32.6 us: local(): w_t = lax.all_gather(w_t, 'z', axis=0, tiled=False)]
    all_to_all x3 -> x2, waiting for transfers between devices: 46.1 us -> 15.5 us  [the longest x1 12.1 us: local(): w_in = lax.all_to_all(master[0].astype(bf16), DP, 0, 0, tiled=True)]
    scatter x3 -> x0, local copies, waits for them, and re-layouts: 19 us -> none  [arrange(): placed = jnp.zeros((blocks, block_width), jnp.float32).at[positions].set(...]
    and x1 -> x0, other arithmetic: 15.7 us -> none  [local(): permuted = jnp.take(context, actual, axis=1)]
    all_to_all x3 -> x2, starting transfers between devices: 23.5 us -> 13.8 us  [the longest x1 9.07 us: local(): w_in = lax.all_to_all(master[0].astype(bf16), DP, 0, 0, tiled=True)]
    transpose x0 -> x2, local copies, waits for them, and re-layouts: none -> 8.49 us  [the longest x1 5.95 us: local(): ct.reshape(n_mp, n_dl, n_z, rows, tokens).transpose(0, 2, 3, 1, 4)]
  transfers between devices with their start and end apart: 7 -> 7, of which waited for: 7 -> 7; matrix products, arithmetic and copies ran while one was open for 13% -> 12% of each run, Pallas kernels for 0% -> 0%
where the time goes in v1:
time: 252 us; the launch traced here: 251 us
  waiting for transfers between devices  121 us (48%)
  blocking collectives  70.1 us (28%)
  between operations  14.7 us (6%)
  starting transfers between devices  14 us (6%)
  local copies, waits for them, and re-layouts  13.5 us (5%)
  matrix products  12.5 us (5%)
  other arithmetic  6.02 us (2%)
    all_to_all x1, blocking collectives, local(): m_in = lax.all_to_all(moments, DP, 0, 0, tiled=True)  39.4 us
    all_gather x1, waiting for transfers between devices, local(): w_t = lax.all_gather(w_t, 'z', axis=0, tiled=False)  32.6 us
    reduce_scatter x1, waiting for transfers between devices, local(): proj_out = lax.psum_scatter(out, DL, scatter_dimension=0, tiled=True)  31.3 us
    all_gather x1, waiting for transfers between devices, local(): og = lax.all_gather(out_grad, DL, axis=0, tiled=True)  22.4 us
    all_to_all x1, blocking collectives, local(): lax.all_to_all(w_t.reshape(n_mp, per_dev, rows, width), MP, 0, 0, tiled=T...  16.6 us
    all_to_all x1, blocking collectives, local(): lax.all_to_all(ct.reshape(n_dl, n_z * rows, tokens), DL, 0, 0, tiled=True)  14.1 us
    all_to_all x1, waiting for transfers between devices, local(): w_in = lax.all_to_all(master[0].astype(bf16), DP, 0, 0, tiled=True)  12.1 us
    reduce_scatter x1, waiting for transfers between devices, local(): lax.psum_scatter(grad.reshape(n_mp, n_z, rows, cols), 'z', scatter_dimens...  9.64 us
  transfers between devices with their start and end apart: 7, of which 7 were waited for; matrix products, arithmetic and copies ran while one was open for 12% of the time, Pallas kernels for 0%

profile of v1, /device:TPU:1, one launch (start us, length us, event | category | flops | bytes accessed | tf_op | source)
XLA Modules:
  0.0 251.5 jit_solution(14708763887175539069)
XLA Ops:
  9.0 14.1 %all_to_all.33 = bf16[4,192,256]{2,1,0:T(8,128)(2,1)} all-to-all(bf16[4,192,256]{2,1,0:T(8,128)(2,1)S(1)} %bitcast.42), channel_id=1, replica_groups=mesh['xh'=2,'z'=8,'c'=2,'xl'=2,'y'=4] {'xh','c'}, dimensions={0} | all-to-all | bytes 786432 | tf_op jit(solution)/shard_map/all_to_all | solution.py:56
  24.0 0.8 convert_element_type.38
  24.8 9.1 %all-to-all-start.1 = ((bf16[32,36,128]{2,1,0:T(8,128)(2,1)}), bf16[32,36,128]{2,1,0:T(8,128)(2,1)S(1)}, u32[]{:S(2)}, u32[]{:S(2)}) async-start(bf16[32,36,128]{2,1,0:T(8,128)(2,1)} %convert_element_type.38), calls=%async_computation.1 | async-start | bytes 655360 | tf_op jit(solution)/shard_map/all_to_all | solution.py:47
  35.2 1.0 subtract_reduce_fusion
  36.3 12.1 %all-to-all-done.1 = bf16[32,36,128]{2,1,0:T(8,128)(2,1)S(1)} async-done(((bf16[32,36,128]{2,1,0:T(8,128)(2,1)}), bf16[32,36,128]{2,1,0:T(8,128)(2,1)S(1)}, u32[]{:S(2)}, u32[]{:S(2)}) %all-to-all-start.1) | async-done | bytes 294944 | tf_op jit(solution)/shard_map/all_to_all | solution.py:47
  48.4 1.0 fusion.4
  49.5 16.6 %all_to_all.34 = bf16[8,6,24,128]{3,2,1,0:T(8,128)(2,1)} all-to-all(bf16[8,6,24,128]{3,2,1,0:T(8,128)(2,1)S(1)} %bitcast.44), channel_id=1, replica_groups=mesh['xh'=2,'z'=8,'c'=2,'xl'=2,'y'=4] {'xl','y'}, dimensions={0} | all-to-all | bytes 589824 | tf_op jit(solution)/shard_map/all_to_all | solution.py:68
  66.1 8.6 %all-gather.8.cloned.1.call-done = bf16[32,192,256]{2,1,0:T(8,128)(2,1)} async-done(((bf16[4,192,256]{2,1,0:T(8,128)(2,1)}), bf16[32,192,256]{2,1,0:T(8,128)(2,1)}) %all-gather.8.cloned.1.call-update) | async-done | bytes 3145744 | tf_op jit(solution)/shard_map/all_gather | solution.py:57
  74.7 5.9 %copy.22 = bf16[8,8,24,4,256]{4,3,2,1,0:T(4,128)(2,1)S(1)} copy(bf16[8,8,24,4,256]{4,2,1,3,0:T(8,128)(2,1)} %bitcast.35) | data formatting | bytes 6291456 | tf_op jit(solution)/shard_map/transpose | solution.py:58
  80.6 0.8 copy.26
  81.4 22.4 %all-gather.6.cloned.1.call-done = bf16[1024,768]{1,0:T(8,128)(2,1)} async-done(((bf16[256,768]{1,0:T(8,128)(2,1)}), bf16[1024,768]{1,0:T(8,128)(2,1)}) %all-gather.6.cloned.1.call-update) | async-done | bytes 1572880 | tf_op jit(solution)/shard_map/all_gather | solution.py:59
  103.7 4.2 %convolution_convert_fusion = bf16[1536,768]{1,0:T(8,128)(2,1)S(1)} fusion(bf16[1536,1024]{1,0:T(8,128)(2,1)S(1)} %bitcast.36, bf16[1024,768]{1,0:T(8,128)(2,1)} %all-gather.6.cloned.1.call-done), kind=kOutput, calls=%fused_computation.4 | convolution fusion | flops 2417098752 | bytes 7077888 | tf_op jit(solution)/shard_map/dot_general | solution.py:61
  107.9 1.6 copy.24
  109.6 32.6 %all-gather.10.cloned.1.call-done = bf16[64,6,24,128]{3,2,1,0:T(8,128)(2,1)} async-done(((bf16[8,6,24,128]{3,2,1,0:T(8,128)(2,1)}), bf16[64,6,24,128]{3,2,1,0:T(8,128)(2,1)}) %all-gather.10.cloned.1.call-update) | async-done | bytes 2359312 | tf_op jit(solution)/shard_map/all_gather | solution.py:69
  142.2 2.5 %copy.23 = bf16[8,8,24,6,128]{4,3,2,1,0:T(8,128)(2,1)S(1)} copy(bf16[8,8,24,6,128]{4,2,3,0,1:T(8,128)(2,1)} %bitcast.41) | data formatting | bytes 4718592 | tf_op jit(solution)/shard_map/transpose | solution.py:70
  144.7 3.9 %fusion.9 = bf16[1024,768]{1,0:T(8,128)(2,1)} fusion(bf16[1536,1024]{1,0:T(8,128)(2,1)S(1)} %bitcast.37, bf16[192,8,6,128]{3,2,1,0:T(8,128)(2,1)S(1)} %bitcast.39), kind=kOutput, calls=%fused_computation.13 | convolution fusion | flops 2416705536 | bytes 7077888 | tf_op jit(solution)/shard_map/dot_general | solution.py:71
  148.6 1.2 convert.12
  150.1 39.4 %all_to_all.35 = bf16[32,36,256]{2,1,0:T(8,128)(2,1)S(1)} all-to-all(bf16[32,36,256]{2,1,0:T(8,128)(2,1)S(1)} %pad_maximum_fusion), channel_id=1, replica_groups=mesh['xh'=2,'z'=8,'c'=2,'xl'=2,'y'=4] {'xh','z','c'}, dimensions={0} | all-to-all | bytes 1179648 | tf_op jit(solution)/shard_map/all_to_all | solution.py:49
  189.6 9.6 %reduce-scatter.5.cloned.1.call-done = bf16[8,1,24,768]{3,2,0,1:T(8,128)(2,1)} async-done(((bf16[8,8,24,768]{3,2,0,1:T(8,128)(2,1)}), bf16[8,1,24,768]{3,2,0,1:T(8,128)(2,1)}) %reduce-scatter.5.cloned.1.call-update) | async-done | bytes 294928 | tf_op jit(solution)/shard_map/reduce_scatter | solution.py:62
  199.2 4.8 %all-to-all-start.4 = ((bf16[8,24,768]{2,1,0:T(8,128)(2,1)}), bf16[8,24,768]{2,1,0:T(8,128)(2,1)S(1)}, u32[]{:S(2)}, u32[]{:S(2)}) async-start(bf16[8,24,768]{2,1,0:T(8,128)(2,1)} %bitcast.43), calls=%async_computation.6 | async-start | bytes 589824 | tf_op jit(solution)/shard_map/all_to_all | solution.py:63
  204.0 2.8 %fusion.1 = f32[1152,384]{1,0:T(8,128)} fusion(s32[1152]{0:T(1024)S(1)} %sub.28, bf16[1152,256]{1,0:T(8,128)(2,1)S(1)} %all_to_all.26, bf16[1152,128]{1,0:T(8,128)(2,1)S(1)} %copy-done.4), kind=kOutput, calls=%fused_computation.3 | convolution fusion | flops 1022312448 | bytes 2658816 | tf_op jit(solution)/shard_map/dot_general | solution.py:74
  206.8 3.4 %all-to-all-done.4 = bf16[8,24,768]{2,1,0:T(8,128)(2,1)S(1)} async-done(((bf16[8,24,768]{2,1,0:T(8,128)(2,1)}), bf16[8,24,768]{2,1,0:T(8,128)(2,1)S(1)}, u32[]{:S(2)}, u32[]{:S(2)}) %all-to-all-start.4) | async-done | bytes 294944 | tf_op jit(solution)/shard_map/all_to_all | solution.py:63
  210.7 2.9 %fusion.20 = (f32[1,1152,128]{2,1,0:T(8,128)}, f32[1,1152,128]{2,1,0:T(8,128)}, f32[1,1152,128]{2,1,0:T(8,128)}) fusion(f32[1152,128]{1,0:T(8,128)S(1)} %reshape.108, f32[1152,384]{1,0:T(8,128)} %fusion.1), kind=kLoop, calls=%fused_computation.27 | loop fusion | flops 2211840 | bytes 4128768 | tf_op jit(solution)/shard_map/broadcast_in_dim | solution.py:79
  213.6 31.3 %reduce-scatter.3.cloned.1.call-done = bf16[256,768]{1,0:T(8,128)(2,1)} async-done(((bf16[1024,768]{1,0:T(8,128)(2,1)}), bf16[256,768]{1,0:T(8,128)(2,1)}) %reduce-scatter.3.cloned.1.call-update) | async-done | bytes 393232 | tf_op jit(solution)/shard_map/reduce_scatter | solution.py:72
  (42 shorter events, 4.3 us)
Async XLA Ops:
  7.2 1.2 copy-start
  7.2 16.8 %copy-start.1 = (f32[1,1152,128]{2,1,0:T(8,128)S(1)}, f32[1,1152,128]{2,1,0:T(8,128)}, u32[]{:S(2)}) copy-start(f32[1,1152,128]{2,1,0:T(8,128)} %param.9) | copy-start | bytes 1769476
  7.2 67.5 %all-gather.8.cloned.1.call-start = ((), (), s32[]{:S(2)}) async-start(), calls=%async_computation.10 | async-start | bytes 3538944 | tf_op jit(solution)/shard_map/all_gather | solution.py:57
  8.4 25.5 %copy-start.5 = (s32[32]{0:T(128)S(1)}, s32[32]{0:T(128)}, u32[]{:S(2)}) copy-start(s32[32]{0:T(128)} %param.12) | copy-start | bytes 388
  23.2 80.6 %all-gather.6.cloned.1.call-start = ((), (), s32[]{:S(2)}) async-start(), calls=%async_computation.8 | async-start | bytes 1966080 | tf_op jit(solution)/shard_map/all_gather | solution.py:59
  24.8 23.6 %all-to-all-start.1 = ((bf16[32,36,128]{2,1,0:T(8,128)(2,1)}), bf16[32,36,128]{2,1,0:T(8,128)(2,1)S(1)}, u32[]{:S(2)}, u32[]{:S(2)}) async-start(bf16[32,36,128]{2,1,0:T(8,128)(2,1)} %convert_element_type.38), calls=%async_computation.1 | async-start | bytes 655360 | tf_op jit(solution)/shard_map/all_to_all | solution.py:47
  33.8 108.4 %all-gather.10.cloned.1.call-start = ((), (), s32[]{:S(2)}) async-start(), calls=%async_computation.11 | async-start | bytes 2654208 | tf_op jit(solution)/shard_map/all_gather | solution.py:69
  48.4 32.2 %copy-start.3 = (bf16[1152,128]{1,0:T(8,128)(2,1)}, bf16[1152,128]{1,0:T(8,128)(2,1)S(1)}, u32[]{:S(2)}) copy-start(bf16[1152,128]{1,0:T(8,128)(2,1)S(1)} %all_to_all.23) | copy-start | bytes 884740
  66.0 133.2 %reduce-scatter.5.cloned.1.call-start = ((), (), s32[]{:S(2)}) async-start(), calls=%async_computation.9 | async-start | bytes 2654208 | tf_op jit(solution)/shard_map/reduce_scatter | solution.py:62
  109.6 135.3 %reduce-scatter.3.cloned.1.call-start = ((), (), s32[]{:S(2)}) async-start(), calls=%async_computation.7 | async-start | bytes 1966080 | tf_op jit(solution)/shard_map/reduce_scatter | solution.py:72
  148.6 1.2 copy-start.2
  150.0 54.0 %copy-start.4 = (bf16[1152,128]{1,0:T(8,128)(2,1)S(1)}, bf16[1152,128]{1,0:T(8,128)(2,1)}, u32[]{:S(2)}) copy-start(bf16[1152,128]{1,0:T(8,128)(2,1)} %copy-done.3) | copy-start | bytes 884740
  199.2 11.0 %all-to-all-start.4 = ((bf16[8,24,768]{2,1,0:T(8,128)(2,1)}), bf16[8,24,768]{2,1,0:T(8,128)(2,1)S(1)}, u32[]{:S(2)}, u32[]{:S(2)}) async-start(bf16[8,24,768]{2,1,0:T(8,128)(2,1)} %bitcast.43), calls=%async_computation.6 | async-start | bytes 589824 | tf_op jit(solution)/shard_map/all_to_all | solution.py:63
Sparse Core Ops, SparseCore 0:
  23.3 51.3 all-gather.7
  76.5 27.2 all-gather.5
  105.5 36.6 all-gather.9
  144.6 54.5 reduce-scatter.4
  202.4 42.4 reduce-scatter.2

commit v2 on v1

v2 whole, which is shorter than its diff:
```python
import jax
import jax.numpy as jnp
from jax import lax
from jax.experimental import pallas as pl
from jax.experimental.pallas import tpu as pltpu
from jax.sharding import Mesh, PartitionSpec as P

beta_one = 0.9
beta_two = 0.999
learn_rate = 0.001
decay_rate = 0.1
epsilon = 1e-08
step_count = 100.0

DP = ("xh", "z", "c")
MP = ("xl", "y")


def adamw(weights, first_moment, second_moment, gradient):
    first_new = beta_one * first_moment + (1.0 - beta_one) * gradient
    second_new = beta_two * second_moment + (1.0 - beta_two) * gradient * gradient
    corrected_first = first_new / (1.0 - beta_one**step_count)
    corrected_second = second_new / (1.0 - beta_two**step_count)
    update = corrected_first / (jnp.sqrt(corrected_second) + epsilon)
    weights_new = weights - learn_rate * (update + decay_rate * weights)
    return (weights_new, first_new, second_new)


def one_hot(index, count):
    rows = lax.broadcasted_iota(jnp.int32, (count, index.shape[0]), 0)
    return (rows == index[None, :]).astype(jnp.bfloat16)


def shift(a, axis, by):
    n = lax.axis_size(axis)
    return lax.ppermute(a, axis, [(i, (i + by) % n) for i in range(n)])


def ring_gather(piece, axis):
    n = lax.axis_size(axis)
    up, down = piece, piece
    got = {0: piece}
    for k in range(1, n // 2):
        up, down = shift(up, axis, 1), shift(down, axis, -1)
        got[n - k], got[k] = up, down
    half = piece.shape[0] // 2
    up, down = shift(up[:half], axis, 1), shift(down[half:], axis, -1)
    got[n // 2] = jnp.concatenate([up, down])
    return [got[k] for k in range(n)]


def add(*terms):
    return sum(t.astype(jnp.float32) for t in terms).astype(terms[0].dtype)


def ring_scatter(part, far_up, far_down, axis, tie):
    n = lax.axis_size(axis)
    h = n // 2
    cut = far_up.shape[2]
    up, down = shift(far_up, axis, 1), shift(far_down, axis, -1)
    up = jnp.concatenate([add(part[h - 1][:, :, :cut], up), part[h - 1][:, :, cut:]], axis=2)
    down = jnp.concatenate([part[h + 1][:, :, :cut], add(part[h + 1][:, :, cut:], down)], axis=2)
    for k in range(h - 1, 0, -1):
        up, down = shift(up, axis, 1), shift(down, axis, -1)
        if k > 1:
            up, down = add(up, part[k - 1]), add(down, part[n - k + 1])
        if k == h - 1:
            up, tie = lax.optimization_barrier((up, tie))
    return add(part[0], up, down), tie


def gradient_parts(order, tiles, outs, n_z):
    n_mp = len(tiles)
    width = tiles[0][0].shape[1]
    rows = sum(t.shape[0] for t in tiles[0]) // n_z
    cols = outs[0].shape[1]
    kind = outs[0].dtype
    flat = [t for tile in tiles for t in tile]
    sizes = [len(tile) for tile in tiles]
    far = n_z // 2

    def body(order_ref, *refs):
        tile_refs, o_refs = list(refs[: len(flat)]), refs[len(flat) : len(flat) + len(outs)]
        g_ref, up_ref, down_ref, t_ref = refs[len(flat) + len(outs) :]
        step = width // len(outs)
        for i in range(n_mp):
            at = order_ref[i]
            k = 0
            for ref in [tile_refs.pop(0) for _ in range(sizes[i])]:
                acc = None
                for j, o_ref in enumerate(o_refs):
                    term = jnp.dot(ref[:, j * step : (j + 1) * step], o_ref[...], preferred_element_type=jnp.float32)
                    acc = term if acc is None else acc + term
                acc = acc.astype(kind)
                for r in range(0, ref.shape[0], rows):
                    piece = acc[r : r + rows]
                    if k == far:
                        up_ref[at] = piece[:, : cols // 2]
                        down_ref[at] = piece[:, cols // 2 :]
                    else:
                        g_ref[k - (k > far), at] = piece
                    t_ref[k, at] = ref[r : r + rows]
                    k += 1

    vmem = pl.BlockSpec(memory_space=pltpu.VMEM)
    g, up, down, tiles_all = pl.pallas_call(
        body,
        out_shape=(
            jax.ShapeDtypeStruct((n_z - 1, n_mp, rows, cols), kind),
            jax.ShapeDtypeStruct((n_mp, rows, cols // 2), kind),
            jax.ShapeDtypeStruct((n_mp, rows, cols // 2), kind),
            jax.ShapeDtypeStruct((n_z, n_mp, rows, width), kind),
        ),
        in_specs=[pl.BlockSpec(memory_space=pltpu.SMEM)] + [vmem] * (len(flat) + len(outs)),
        out_specs=(vmem,) * 4,
        name="gradient_parts",
    )(order, *flat, *outs)
    return {k: g[k - (k > far)] for k in range(n_z) if k != far}, up, down, tiles_all


def local(context, out_grad, master, moment_one, moment_two, new_owner, old_pieces):
    f32, bf16 = jnp.float32, jnp.bfloat16
    n_dp, n_mp, n_z, n_y = lax.axis_size(DP), lax.axis_size(MP), lax.axis_size("z"), lax.axis_size("y")
    d, xh, z, c = lax.axis_index(DP), lax.axis_index("xh"), lax.axis_index("z"), lax.axis_index("c")
    xl, y = lax.axis_index("xl"), lax.axis_index("y")
    blocks, width = master.shape[1:]
    tokens, cols = context.shape
    per_dev = cols // width
    per_row = per_dev * n_mp
    rows = blocks // per_row
    own_slab = new_owner[d]
    positions = (lax.dynamic_index_in_dim(old_pieces, d, 1, keepdims=False) - own_slab * blocks).reshape(-1)
    rel = jnp.arange(n_mp, dtype=jnp.int32)
    mp_of_rel = (rel // n_y ^ xl) * n_y + (rel % n_y + y) % n_y

    states = jnp.concatenate([master[0], moment_one[0], moment_two[0]], axis=1).astype(bf16)
    states = lax.all_to_all(states, DP, 0, 0, tiled=True)

    spot = jnp.arange(cols, dtype=jnp.int32)
    slab = spot // rows
    dp_of = ((slab // (2 * n_z) ^ xh) * n_z + (slab % n_z + z) % n_z) * 2 + (slab // n_z % 2 ^ c)
    hit = dp_of[:, None] == jnp.arange(n_dp, dtype=jnp.int32)[None]
    wanted = jnp.sum(jnp.where(hit, new_owner[None], 0), axis=1, keepdims=True) * rows + (spot % rows)[:, None]
    select = (lax.broadcasted_iota(jnp.int32, (cols, cols), 1) == wanted).astype(bf16)
    ct = lax.dot_general(select, context, (((1,), (1,)), ((), ())), preferred_element_type=f32).astype(bf16)
    half = cols // 2
    quarter = half // 2
    ct_x = shift(ct[half:], "xh", 1)
    ct_a = jnp.concatenate([ct[:quarter], ct_x[:quarter]], axis=1)
    ct_b = shift(jnp.concatenate([ct[quarter:half], ct_x[quarter:]], axis=1), "c", 1)
    og_x = shift(out_grad, "xh", 1)
    og_c, og_xc = shift(out_grad, "c", 1), shift(og_x, "c", 1)

    tile = jnp.concatenate([ct_a, ct_b], axis=1)
    cut = quarter // 2
    tiles = []
    for own in (tile, shift(tile, "xl", 1)):
        up, down = shift(own, "y", 1), shift(own, "y", -1)
        far = [shift(down[:cut], "y", -1), shift(up[cut:], "y", 1)]
        tiles += [[own], [down], far, [up]]

    w_at = (positions % per_row) * rows + positions // per_row
    w_t = jnp.dot(one_hot(w_at, blocks), states[:, :width], preferred_element_type=f32).astype(bf16)
    w_t = lax.all_to_all(w_t.reshape(n_mp, per_dev, rows, width), MP, 0, 0, tiled=True)
    w_t = w_t.transpose(0, 2, 1, 3).reshape(n_mp, rows, cols)
    placed = jnp.dot(one_hot(positions, blocks), states, preferred_element_type=f32)
    grads, far_up, far_down, ct_all = gradient_parts(mp_of_rel, tiles, [out_grad, og_x, og_c, og_xc], n_z)
    w_all = jnp.concatenate(ring_gather(w_t, "z")).reshape(n_z * n_mp * rows, cols)

    grad, placed = ring_scatter(grads, far_up, far_down, "z", placed)
    grad = lax.all_to_all(grad, MP, 0, 0, tiled=True)
    grad = grad.reshape(n_mp, rows, per_dev, width).transpose(1, 0, 2, 3).reshape(blocks, width).astype(f32)

    ct_all = ct_all.reshape(n_z * n_mp * rows, 4 * tokens)
    first = lax.dot_general(ct_all[:, 2 * tokens :], w_all, (((0,), (0,)), ((), ())), preferred_element_type=f32)
    first = shift(first.astype(bf16), "c", 1)
    mine = lax.dot_general(ct_all[:, : 2 * tokens], w_all, (((0,), (0,)), ((), ())), preferred_element_type=f32)
    mine = lax.optimization_barrier(mine)
    partner = shift(add(first[tokens:], mine[tokens:]), "xh", 1)
    proj_out = add(first[:tokens], mine[:tokens], partner)

    weights, first_moment, second_moment = (placed[:, i * width : (i + 1) * width] for i in range(3))
    weights_new, first_new, second_new = adamw(weights, first_moment, second_moment, grad)
    return (proj_out, weights_new[None], first_new[None], second_new[None])


def solution(mesh):
    fine = Mesh(mesh.devices.reshape(2, 8, 2, 2, 4), DP + MP)
    placed = (P(DP, MP), P(DP, MP), P(MP, DP, None), P(MP, DP, None), P(MP, DP, None), P(), P())
    return jax.shard_map(
        local,
        mesh=fine,
        in_specs=placed,
        out_specs=(P(DP, MP), P(MP, DP, None), P(MP, DP, None), P(MP, DP, None)),
        check_vma=False,
    )
```

time: 252 us -> 176 us (0.70)
  blocking collectives: 70.1 us -> 11.5 us
  waiting for transfers between devices: 121 us -> 64.8 us
  starting transfers between devices: 14 us -> 67.7 us
  between operations: 14.7 us -> 1.9 us
  local copies, waits for them, and re-layouts: 13.5 us -> 3.09 us
  Pallas kernels: 0 us -> 7.53 us
    all_gather x3 -> x0, waiting for transfers between devices: 63.5 us -> none  [the longest x1 32.6 us: local(): w_t = lax.all_gather(w_t, 'z', axis=0, tiled=False)]
    ppermute x0 -> x32, waiting for transfers between devices: none -> 61.4 us  [shift(): return lax.ppermute(a, axis, [(i, (i + by) % n) for i in range(n)])]
    all_to_all x3 -> x1, blocking collectives: 70.1 us -> 11.5 us  [local(): grad = lax.all_to_all(grad, MP, 0, 0, tiled=True)]
    ppermute x0 -> x32, starting transfers between devices: none -> 53.8 us  [shift(): return lax.ppermute(a, axis, [(i, (i + by) % n) for i in range(n)])]
    reduce_scatter x2 -> x0, waiting for transfers between devices: 41 us -> none  [the longest x1 31.3 us: local(): proj_out = lax.psum_scatter(out, DL, scatter_dimension=0, tiled=True)]
    all_to_all x2, waiting for transfers between devices: 15.5 us -> 3.32 us  [the longest x1 3.32 us: local(): lax.all_to_all(w_t.reshape(n_mp, per_dev, rows, width), MP, 0, 0, tiled=T...]
    transpose x2 -> x0, local copies, waits for them, and re-layouts: 8.49 us -> none  [the longest x1 5.95 us: local(): ct.reshape(n_mp, n_dl, n_z, rows, tokens).transpose(0, 2, 3, 1, 4)]
    pallas_call x0 -> x1, Pallas kernels: none -> 7.53 us  [gradient_parts(): pl.pallas_call(body, out_shape=(jax.ShapeDtypeStruct((n_z - 1, n_mp, rows...]
  transfers between devices with their start and end apart: 7 -> 34, of which waited for: 7 -> 15; matrix products, arithmetic and copies ran while one was open for 12% -> 10% of each run, Pallas kernels for 0% -> 4%
where the time goes in v2:
time: 176 us; the launch traced here: 173 us
  starting transfers between devices  67.7 us (38%)
  waiting for transfers between devices  64.8 us (37%)
  blocking collectives  11.5 us (7%)
  matrix products  10.3 us (6%)
  Pallas kernels  7.53 us (4%)
  other arithmetic  6.67 us (4%)
  local copies, waits for them, and re-layouts  3.09 us (2%)
  between operations  1.9 us (1%)
    ppermute x32, waiting for transfers between devices, shift(): return lax.ppermute(a, axis, [(i, (i + by) % n) for i in range(n)])  61.4 us
    ppermute x32, starting transfers between devices, shift(): return lax.ppermute(a, axis, [(i, (i + by) % n) for i in range(n)])  53.8 us
    all_to_all x1, blocking collectives, local(): grad = lax.all_to_all(grad, MP, 0, 0, tiled=True)  11.5 us
    all_to_all x1, starting transfers between devices, local(): states = lax.all_to_all(states, DP, 0, 0, tiled=True)  10.5 us
    pallas_call x1, Pallas kernels, gradient_parts(): pl.pallas_call(body, out_shape=(jax.ShapeDtypeStruct((n_z - 1, n_mp, rows...  7.53 us
    dot_general x1, matrix products, local(): lax.dot_general(ct_all[:, :2 * tokens], w_all, (((0,), (0,)), ((), ())),...  3.7 us
  transfers between devices with their start and end apart: 34, of which 15 were waited for; matrix products, arithmetic and copies ran while one was open for 10% of the time, Pallas kernels for 4%

profile of v2, /device:TPU:1, one launch (start us, length us, event | category | flops | bytes accessed | tf_op | source)
XLA Modules:
  0.0 173.4 jit_solution(4955928681670087708)
XLA Ops:
  2.2 3.7 %collective-permute-start = (bf16[384,256]{1,0:T(8,128)(2,1)S(1)}, bf16[384,256]{1,0:T(8,128)(2,1)S(1)}, u32[]{:S(2)}, u32[]{:S(2)}) collective-permute-start(bf16[384,256]{1,0:T(8,128)(2,1)S(1)} %slice.129), channel_id=1, source_target_pairs={{0,128},{128,0},{1,129},{129,1},{2,130},{130,2},{3,131},{131,3},{4... | collective-permute-start | bytes 589832 | tf_op jit(solution)/shard_map/ppermute | solution.py:36
  5.9 3.6 %collective-permute-done = bf16[384,256]{1,0:T(8,128)(2,1)S(1)} collective-permute-done((bf16[384,256]{1,0:T(8,128)(2,1)S(1)}, bf16[384,256]{1,0:T(8,128)(2,1)S(1)}, u32[]{:S(2)}, u32[]{:S(2)}) %collective-permute-start) | collective-permute-done | bytes 196640 | tf_op jit(solution)/shard_map/ppermute | solution.py:36
  9.5 3.3 %collective-permute-start.1 = (bf16[192,512]{1,0:T(8,128)(2,1)S(1)}, bf16[192,512]{1,0:T(8,128)(2,1)S(1)}, u32[]{:S(2)}, u32[]{:S(2)}) collective-permute-start(bf16[192,512]{1,0:T(8,128)(2,1)S(1)} %pad_maximum_fusion.4), channel_id=1, source_target_pairs={{0,8},{8,0},{1,9},{9,1},{2,10},{10,2},{3,11},{11,3},{4,12},{12,4},... | collective-permute-start | bytes 589832 | tf_op jit(solution)/shard_map/ppermute | solution.py:36
  14.3 10.5 %all-to-all-start = ((bf16[32,36,384]{2,1,0:T(8,128)(2,1)}), bf16[32,36,384]{2,1,0:T(8,128)(2,1)S(1)}, u32[]{:S(2)}, u32[]{:S(2)}) async-start(bf16[32,36,384]{2,1,0:T(8,128)(2,1)} %pad_maximum_fusion), calls=%async_computation | async-start | bytes 1966080 | tf_op jit(solution)/shard_map/all_to_all | solution.py:137
  25.2 3.5 %collective-permute-start.11 = (bf16[256,768]{1,0:T(8,128)(2,1)}, bf16[256,768]{1,0:T(8,128)(2,1)}, u32[]{:S(2)}, u32[]{:S(2)}) collective-permute-start(bf16[256,768]{1,0:T(8,128)(2,1)} %refs_10_.1), channel_id=1, source_target_pairs={{0,128},{128,0},{1,129},{129,1},{2,130},{130,2},{3,131},{131,3},{4... | collective-permute-start | bytes 1179656 | tf_op jit(solution)/shard_map/ppermute | solution.py:36
  31.4 10.5 %collective-permute-done.6.refs_5_ = bf16[192,1024]{1,0:T(8,128)(2,1)} collective-permute-done((bf16[192,1024]{1,0:T(8,128)(2,1)S(1)}, bf16[192,1024]{1,0:T(8,128)(2,1)}, u32[]{:S(2)}, u32[]{:S(2)}) %collective-permute-start.6) | collective-permute-done | bytes 393248 | tf_op jit(solution)/shard_map/ppermute | solution.py:36
  44.6 11.3 %collective-permute-done.11.refs_11_ = bf16[256,768]{1,0:T(8,128)(2,1)} collective-permute-done((bf16[256,768]{1,0:T(8,128)(2,1)}, bf16[256,768]{1,0:T(8,128)(2,1)}, u32[]{:S(2)}, u32[]{:S(2)}) %collective-permute-start.11) | collective-permute-done | bytes 393248 | tf_op jit(solution)/shard_map/ppermute | solution.py:36
  59.8 2.8 %collective-permute-start.3 = (bf16[96,1024]{1,0:T(8,128)(2,1)S(1)}, bf16[96,1024]{1,0:T(8,128)(2,1)S(1)}, u32[]{:S(2)}, u32[]{:S(2)}) collective-permute-start(bf16[96,1024]{1,0:T(8,128)(2,1)S(1)} %slice.133), channel_id=1, source_target_pairs={{0,3},{1,0},{2,1},{3,2},{4,7},{5,4},{6,5},{7,6},{8,11},{9,8},{10,9... | collective-permute-start | bytes 589832 | tf_op jit(solution)/shard_map/ppermute | solution.py:36
  62.9 2.9 %collective-permute-start.8 = (bf16[96,1024]{1,0:T(8,128)(2,1)S(1)}, bf16[96,1024]{1,0:T(8,128)(2,1)}, u32[]{:S(2)}, u32[]{:S(2)}) collective-permute-start(bf16[96,1024]{1,0:T(8,128)(2,1)S(1)} %slice.135), channel_id=1, source_target_pairs={{0,3},{1,0},{2,1},{3,2},{4,7},{5,4},{6,5},{7,6},{8,11},{9,8},{10,9... | collective-permute-start | bytes 589832 | tf_op jit(solution)/shard_map/ppermute | solution.py:36
  66.5 3.3 %collective-permute-done.5.refs_3_ = bf16[96,1024]{1,0:T(8,128)(2,1)} collective-permute-done((bf16[96,1024]{1,0:T(8,128)(2,1)S(1)}, bf16[96,1024]{1,0:T(8,128)(2,1)}, u32[]{:S(2)}, u32[]{:S(2)}) %collective-permute-start.5) | collective-permute-done | bytes 196640 | tf_op jit(solution)/shard_map/ppermute | solution.py:36
  69.8 4.2 %collective-permute-done.10.refs_8_ = bf16[96,1024]{1,0:T(8,128)(2,1)} collective-permute-done((bf16[96,1024]{1,0:T(8,128)(2,1)S(1)}, bf16[96,1024]{1,0:T(8,128)(2,1)}, u32[]{:S(2)}, u32[]{:S(2)}) %collective-permute-start.10) | collective-permute-done | bytes 196640 | tf_op jit(solution)/shard_map/ppermute | solution.py:36
  74.1 7.5 %gradient_parts.1 = (bf16[7,8,24,768]{3,2,1,0:T(8,128)(2,1)}, bf16[8,24,384]{2,1,0:T(8,128)(2,1)}, bf16[8,24,384]{2,1,0:T(8,128)(2,1)}, bf16[8,8,24,1024]{3,2,1,0:T(8,128)(2,1)}) custom-call(s32[8]{0:T(128)} %fusion.52.order_ref, bf16[192,1024]{1,0:T(8,128)(2,1)} %copy-done.4, bf16[192,1024]{1,0:T(8,128)(2,1)} %copy-done.5, bf16[96,1024]{1,0:T(8,128)(2,1)} %copy-done.13, ...), custom_call_target="tpu_custom_call" | custom-call | tf_op jit(solution)/shard_map/gradient_parts/pallas_call | solution.py:106
  89.1 3.4 %all-to-all-start.1 = ((bf16[8,6,24,128]{3,2,1,0:T(8,128)(2,1)}), bf16[8,6,24,128]{3,2,1,0:T(8,128)(2,1)S(1)}, u32[]{:S(2)}, u32[]{:S(2)}) async-start(bf16[8,6,24,128]{3,2,1,0:T(8,128)(2,1)} %bitcast.2), calls=%async_computation.1 | async-start | bytes 589824 | tf_op jit(solution)/shard_map/all_to_all | solution.py:164
  95.4 3.3 %all-to-all-done.1 = bf16[8,6,24,128]{3,2,1,0:T(8,128)(2,1)S(1)} async-done(((bf16[8,6,24,128]{3,2,1,0:T(8,128)(2,1)}), bf16[8,6,24,128]{3,2,1,0:T(8,128)(2,1)S(1)}, u32[]{:S(2)}, u32[]{:S(2)}) %all-to-all-start.1) | async-done | bytes 294944 | tf_op jit(solution)/shard_map/all_to_all | solution.py:164
  101.4 2.8 %fusion.1 = f32[1152,384]{1,0:T(8,128)} fusion(bf16[1152,384]{1,0:T(8,128)(2,1)S(1)} %all_to_all.13, s32[1152]{0:T(1024)S(1)} %sub.54), kind=kOutput, calls=%fused_computation.3 | convolution fusion | flops 1020542976 | bytes 2658816 | tf_op jit(solution)/shard_map/dot_general | solution.py:166
  105.6 3.1 %collective-permute-start.15 = (bf16[8,24,768]{2,1,0:T(8,128)(2,1)S(1)}, bf16[8,24,768]{2,1,0:T(8,128)(2,1)S(1)}, u32[]{:S(2)}, u32[]{:S(2)}) collective-permute-start(bf16[8,24,768]{2,1,0:T(8,128)(2,1)S(1)} %collective-permute-done.14), channel_id=1, source_target_pairs={{0,112},{16,0},{32,16},{48,32},{64,48},{80,64},{96,80},{112,96},{1... | collective-permute-start | bytes 884744 | tf_op jit(solution)/shard_map/ppermute | solution.py:36
  112.9 3.1 %collective-permute-start.16 = (bf16[8,24,768]{2,1,0:T(8,128)(2,1)S(1)}, bf16[8,24,768]{2,1,0:T(8,128)(2,1)S(1)}, u32[]{:S(2)}, u32[]{:S(2)}) collective-permute-start(bf16[8,24,768]{2,1,0:T(8,128)(2,1)S(1)} %collective-permute-done.15), channel_id=1, source_target_pairs={{0,112},{16,0},{32,16},{48,32},{64,48},{80,64},{96,80},{112,96},{1... | collective-permute-start | bytes 884744 | tf_op jit(solution)/shard_map/ppermute | solution.py:36
  116.3 4.3 %collective-permute-done.26 = bf16[8,24,768]{2,1,0:T(8,128)(2,1)S(1)} collective-permute-done((bf16[8,24,768]{2,1,0:T(8,128)(2,1)S(1)}, bf16[8,24,768]{2,1,0:T(8,128)(2,1)S(1)}, u32[]{:S(2)}, u32[]{:S(2)}) %collective-permute-start.26) | collective-permute-done | bytes 294944 | tf_op jit(solution)/shard_map/ppermute | solution.py:36
  123.5 3.4 %collective-permute-done.19 = bf16[8,24,768]{2,1,0:T(8,128)(2,1)S(1)} collective-permute-done((bf16[8,24,768]{2,1,0:T(8,128)(2,1)S(1)}, bf16[8,24,768]{2,1,0:T(8,128)(2,1)S(1)}, u32[]{:S(2)}, u32[]{:S(2)}) %collective-permute-start.19) | collective-permute-done | bytes 294944 | tf_op jit(solution)/shard_map/ppermute | solution.py:36
  129.8 6.6 %collective-permute-done.20 = bf16[4,24,768]{2,1,0:T(8,128)(2,1)S(1)} collective-permute-done((bf16[4,24,768]{2,1,0:T(8,128)(2,1)S(1)}, bf16[4,24,768]{2,1,0:T(8,128)(2,1)S(1)}, u32[]{:S(2)}, u32[]{:S(2)}) %collective-permute-start.20) | collective-permute-done | bytes 147488 | tf_op jit(solution)/shard_map/ppermute | solution.py:36
  138.0 7.7 %collective-permute-start.22 = (bf16[512,768]{1,0:T(8,128)(2,1)S(1)}, bf16[512,768]{1,0:T(8,128)(2,1)S(1)}, u32[]{:S(2)}, u32[]{:S(2)}) collective-permute-start(bf16[512,768]{1,0:T(8,128)(2,1)S(1)} %fusion.10), channel_id=1, source_target_pairs={{0,8},{8,0},{1,9},{9,1},{2,10},{10,2},{3,11},{11,3},{4,12},{12,4},... | collective-permute-start | bytes 2359304 | tf_op jit(solution)/shard_map/ppermute | solution.py:36
  145.8 11.5 %all_to_all.19 = bf16[8,24,768]{2,1,0:T(8,128)(2,1)S(1)} all-to-all(bf16[8,24,768]{2,1,0:T(8,128)(2,1)S(1)} %fusion.23), channel_id=1, replica_groups=mesh['xh'=2,'z'=8,'c'=2,'xl'=2,'y'=4] {'xl','y'}, dimensions={0} | all-to-all | bytes 589824 | tf_op jit(solution)/shard_map/all_to_all | solution.py:171
  157.7 3.7 %fusion.6 = f32[512,768]{1,0:T(8,128)S(1)} fusion(bf16[1536,768]{1,0:T(8,128)(2,1)} %bitcast.46, bf16[1536,1024]{1,0:T(8,128)(2,1)} %bitcast.47), kind=kOutput, calls=%fused_computation.9 | convolution fusion | flops 1207959552 | bytes 5505024 | tf_op jit(solution)/shard_map/dot_general | solution.py:177
  163.3 9.2 %collective-permute-done.23 = bf16[256,768]{1,0:T(8,128)(2,1)S(1)} collective-permute-done((bf16[256,768]{1,0:T(8,128)(2,1)S(1)}, bf16[256,768]{1,0:T(8,128)(2,1)S(1)}, u32[]{:S(2)}, u32[]{:S(2)}) %collective-permute-start.23) | collective-permute-done | bytes 393248 | tf_op jit(solution)/shard_map/ppermute | solution.py:36
  (134 shorter events, 42.3 us)
Async XLA Ops:
  9.5 15.2 %collective-permute-start.1 = (bf16[192,512]{1,0:T(8,128)(2,1)S(1)}, bf16[192,512]{1,0:T(8,128)(2,1)S(1)}, u32[]{:S(2)}, u32[]{:S(2)}) collective-permute-start(bf16[192,512]{1,0:T(8,128)(2,1)S(1)} %pad_maximum_fusion.4), channel_id=1, source_target_pairs={{0,8},{8,0},{1,9},{9,1},{2,10},{10,2},{3,11},{11,3},{4,12},{12,4},... | collective-permute-start | bytes 589832 | tf_op jit(solution)/shard_map/ppermute | solution.py:36
  14.3 72.9 %all-to-all-start = ((bf16[32,36,384]{2,1,0:T(8,128)(2,1)}), bf16[32,36,384]{2,1,0:T(8,128)(2,1)S(1)}, u32[]{:S(2)}, u32[]{:S(2)}) async-start(bf16[32,36,384]{2,1,0:T(8,128)(2,1)} %pad_maximum_fusion), calls=%async_computation | async-start | bytes 1966080 | tf_op jit(solution)/shard_map/all_to_all | solution.py:137
  24.8 17.1 %collective-permute-start.6 = (bf16[192,1024]{1,0:T(8,128)(2,1)S(1)}, bf16[192,1024]{1,0:T(8,128)(2,1)}, u32[]{:S(2)}, u32[]{:S(2)}) collective-permute-start(bf16[192,1024]{1,0:T(8,128)(2,1)S(1)} %pad_maximum_fusion.1.refs_0_), channel_id=1, source_target_pairs={{0,4},{4,0},{1,5},{5,1},{2,6},{6,2},{3,7},{7,3},{8,12},{12,8},{9,1... | collective-permute-start | bytes 1179656 | tf_op jit(solution)/shard_map/ppermute | solution.py:36
  25.2 30.7 %collective-permute-start.11 = (bf16[256,768]{1,0:T(8,128)(2,1)}, bf16[256,768]{1,0:T(8,128)(2,1)}, u32[]{:S(2)}, u32[]{:S(2)}) collective-permute-start(bf16[256,768]{1,0:T(8,128)(2,1)} %refs_10_.1), channel_id=1, source_target_pairs={{0,128},{128,0},{1,129},{129,1},{2,130},{130,2},{3,131},{131,3},{4... | collective-permute-start | bytes 1179656 | tf_op jit(solution)/shard_map/ppermute | solution.py:36
  28.7 28.2 %collective-permute-start.2 = (bf16[192,1024]{1,0:T(8,128)(2,1)S(1)}, bf16[192,1024]{1,0:T(8,128)(2,1)S(1)}, u32[]{:S(2)}, u32[]{:S(2)}) collective-permute-start(bf16[192,1024]{1,0:T(8,128)(2,1)S(1)} %pad_maximum_fusion.1.refs_0_), channel_id=1, source_target_pairs={{0,3},{1,0},{2,1},{3,2},{4,7},{5,4},{6,5},{7,6},{8,11},{9,8},{10,9... | collective-permute-start | bytes 1179656 | tf_op jit(solution)/shard_map/ppermute | solution.py:36
  31.4 28.4 %collective-permute-start.4 = (bf16[192,1024]{1,0:T(8,128)(2,1)S(1)}, bf16[192,1024]{1,0:T(8,128)(2,1)S(1)}, u32[]{:S(2)}, u32[]{:S(2)}) collective-permute-start(bf16[192,1024]{1,0:T(8,128)(2,1)S(1)} %pad_maximum_fusion.1.refs_0_), channel_id=1, source_target_pairs={{0,1},{1,2},{2,3},{3,0},{4,5},{5,6},{6,7},{7,4},{8,9},{9,10},{10,1... | collective-permute-start | bytes 1179656 | tf_op jit(solution)/shard_map/ppermute | solution.py:36
  41.9 20.8 %collective-permute-start.9 = (bf16[192,1024]{1,0:T(8,128)(2,1)}, bf16[192,1024]{1,0:T(8,128)(2,1)S(1)}, u32[]{:S(2)}, u32[]{:S(2)}) collective-permute-start(bf16[192,1024]{1,0:T(8,128)(2,1)} %collective-permute-done.6.refs_5_), channel_id=1, source_target_pairs={{0,1},{1,2},{2,3},{3,0},{4,5},{5,6},{6,7},{7,4},{8,9},{9,10},{10,1... | collective-permute-start | bytes 1179656 | tf_op jit(solution)/shard_map/ppermute | solution.py:36
  43.2 19.6 %collective-permute-start.7 = (bf16[192,1024]{1,0:T(8,128)(2,1)}, bf16[192,1024]{1,0:T(8,128)(2,1)S(1)}, u32[]{:S(2)}, u32[]{:S(2)}) collective-permute-start(bf16[192,1024]{1,0:T(8,128)(2,1)} %collective-permute-done.6.refs_5_), channel_id=1, source_target_pairs={{0,3},{1,0},{2,1},{3,2},{4,7},{5,4},{6,5},{7,6},{8,11},{9,8},{10,9... | collective-permute-start | bytes 1179656 | tf_op jit(solution)/shard_map/ppermute | solution.py:36
  56.9 9.0 %collective-permute-start.13 = (bf16[256,768]{1,0:T(8,128)(2,1)}, bf16[256,768]{1,0:T(8,128)(2,1)}, u32[]{:S(2)}, u32[]{:S(2)}) collective-permute-start(bf16[256,768]{1,0:T(8,128)(2,1)} %collective-permute-done.11.refs_11_), channel_id=1, source_target_pairs={{0,8},{8,0},{1,9},{9,1},{2,10},{10,2},{3,11},{11,3},{4,12},{12,4},... | collective-permute-start | bytes 1179656 | tf_op jit(solution)/shard_map/ppermute | solution.py:36
  62.8 11.2 %collective-permute-start.10 = (bf16[96,1024]{1,0:T(8,128)(2,1)S(1)}, bf16[96,1024]{1,0:T(8,128)(2,1)}, u32[]{:S(2)}, u32[]{:S(2)}) collective-permute-start(bf16[96,1024]{1,0:T(8,128)(2,1)S(1)} %slice.136), channel_id=1, source_target_pairs={{0,1},{1,2},{2,3},{3,0},{4,5},{5,6},{6,7},{7,4},{8,9},{9,10},{10,1... | collective-permute-start | bytes 589832 | tf_op jit(solution)/shard_map/ppermute | solution.py:36
  62.9 11.1 %collective-permute-start.8 = (bf16[96,1024]{1,0:T(8,128)(2,1)S(1)}, bf16[96,1024]{1,0:T(8,128)(2,1)}, u32[]{:S(2)}, u32[]{:S(2)}) collective-permute-start(bf16[96,1024]{1,0:T(8,128)(2,1)S(1)} %slice.135), channel_id=1, source_target_pairs={{0,3},{1,0},{2,1},{3,2},{4,7},{5,4},{6,5},{7,6},{8,11},{9,8},{10,9... | collective-permute-start | bytes 589832 | tf_op jit(solution)/shard_map/ppermute | solution.py:36
  87.1 17.1 %collective-permute-start.25 = (bf16[8,24,768]{2,1,0:T(8,128)(2,1)S(1)}, bf16[8,24,768]{2,1,0:T(8,128)(2,1)S(1)}, u32[]{:S(2)}, u32[]{:S(2)}) collective-permute-start(bf16[8,24,768]{2,1,0:T(8,128)(2,1)S(1)} %pad_maximum_fusion.2), channel_id=1, source_target_pairs={{0,16},{16,32},{32,48},{48,64},{64,80},{80,96},{96,112},{112,0},{1... | collective-permute-start | bytes 884744 | tf_op jit(solution)/shard_map/ppermute | solution.py:36
  89.1 9.6 %all-to-all-start.1 = ((bf16[8,6,24,128]{3,2,1,0:T(8,128)(2,1)}), bf16[8,6,24,128]{3,2,1,0:T(8,128)(2,1)S(1)}, u32[]{:S(2)}, u32[]{:S(2)}) async-start(bf16[8,6,24,128]{3,2,1,0:T(8,128)(2,1)} %bitcast.2), calls=%async_computation.1 | async-start | bytes 589824 | tf_op jit(solution)/shard_map/all_to_all | solution.py:164
  92.6 11.6 %collective-permute-start.29 = (bf16[8,24,768]{2,1,0:T(8,128)(2,1)S(1)}, bf16[8,24,768]{2,1,0:T(8,128)(2,1)S(1)}, u32[]{:S(2)}, u32[]{:S(2)}) collective-permute-start(bf16[8,24,768]{2,1,0:T(8,128)(2,1)S(1)} %pad_maximum_fusion.3), channel_id=1, source_target_pairs={{0,112},{16,0},{32,16},{48,32},{64,48},{80,64},{96,80},{112,96},{1... | collective-permute-start | bytes 884744 | tf_op jit(solution)/shard_map/ppermute | solution.py:36
  108.8 11.8 %collective-permute-start.26 = (bf16[8,24,768]{2,1,0:T(8,128)(2,1)S(1)}, bf16[8,24,768]{2,1,0:T(8,128)(2,1)S(1)}, u32[]{:S(2)}, u32[]{:S(2)}) collective-permute-start(bf16[8,24,768]{2,1,0:T(8,128)(2,1)S(1)} %get-tuple-element.14), channel_id=1, source_target_pairs={{0,16},{16,32},{32,48},{48,64},{64,80},{80,96},{96,112},{112,0},{1... | collective-permute-start | bytes 884744 | tf_op jit(solution)/shard_map/ppermute | solution.py:36
  109.4 11.2 %collective-permute-start.30 = (bf16[8,24,768]{2,1,0:T(8,128)(2,1)S(1)}, bf16[8,24,768]{2,1,0:T(8,128)(2,1)S(1)}, u32[]{:S(2)}, u32[]{:S(2)}) collective-permute-start(bf16[8,24,768]{2,1,0:T(8,128)(2,1)S(1)} %get-tuple-element.21), channel_id=1, source_target_pairs={{0,112},{16,0},{32,16},{48,32},{64,48},{80,64},{96,80},{112,96},{1... | collective-permute-start | bytes 884744 | tf_op jit(solution)/shard_map/ppermute | solution.py:36
  112.9 14.1 %collective-permute-start.16 = (bf16[8,24,768]{2,1,0:T(8,128)(2,1)S(1)}, bf16[8,24,768]{2,1,0:T(8,128)(2,1)S(1)}, u32[]{:S(2)}, u32[]{:S(2)}) collective-permute-start(bf16[8,24,768]{2,1,0:T(8,128)(2,1)S(1)} %collective-permute-done.15), channel_id=1, source_target_pairs={{0,112},{16,0},{32,16},{48,32},{64,48},{80,64},{96,80},{112,96},{1... | collective-permute-start | bytes 884744 | tf_op jit(solution)/shard_map/ppermute | solution.py:36
  116.3 10.6 %collective-permute-start.19 = (bf16[8,24,768]{2,1,0:T(8,128)(2,1)S(1)}, bf16[8,24,768]{2,1,0:T(8,128)(2,1)S(1)}, u32[]{:S(2)}, u32[]{:S(2)}) collective-permute-start(bf16[8,24,768]{2,1,0:T(8,128)(2,1)S(1)} %collective-permute-done.18), channel_id=1, source_target_pairs={{0,16},{16,32},{32,48},{48,64},{64,80},{80,96},{96,112},{112,0},{1... | collective-permute-start | bytes 884744 | tf_op jit(solution)/shard_map/ppermute | solution.py:36
  120.7 25.0 %collective-permute-start.27 = (bf16[8,24,768]{2,1,0:T(8,128)(2,1)S(1)}, bf16[8,24,768]{2,1,0:T(8,128)(2,1)S(1)}, u32[]{:S(2)}, u32[]{:S(2)}) collective-permute-start(bf16[8,24,768]{2,1,0:T(8,128)(2,1)S(1)} %get-tuple-element.19), channel_id=1, source_target_pairs={{0,16},{16,32},{32,48},{48,64},{64,80},{80,96},{96,112},{112,0},{1... | collective-permute-start | bytes 884744 | tf_op jit(solution)/shard_map/ppermute | solution.py:36
  122.0 23.7 %collective-permute-start.31 = (bf16[8,24,768]{2,1,0:T(8,128)(2,1)S(1)}, bf16[8,24,768]{2,1,0:T(8,128)(2,1)S(1)}, u32[]{:S(2)}, u32[]{:S(2)}) collective-permute-start(bf16[8,24,768]{2,1,0:T(8,128)(2,1)S(1)} %get-tuple-element.20), channel_id=1, source_target_pairs={{0,112},{16,0},{32,16},{48,32},{64,48},{80,64},{96,80},{112,96},{1... | collective-permute-start | bytes 884744 | tf_op jit(solution)/shard_map/ppermute | solution.py:36
  126.9 9.5 %collective-permute-start.20 = (bf16[4,24,768]{2,1,0:T(8,128)(2,1)S(1)}, bf16[4,24,768]{2,1,0:T(8,128)(2,1)S(1)}, u32[]{:S(2)}, u32[]{:S(2)}) collective-permute-start(bf16[4,24,768]{2,1,0:T(8,128)(2,1)S(1)} %slice.139), channel_id=1, source_target_pairs={{0,16},{16,32},{32,48},{48,64},{64,80},{80,96},{96,112},{112,0},{1... | collective-permute-start | bytes 442376 | tf_op jit(solution)/shard_map/ppermute | solution.py:36
  127.0 9.3 %collective-permute-start.21 = (bf16[4,24,768]{2,1,0:T(8,128)(2,1)S(1)}, bf16[4,24,768]{2,1,0:T(8,128)(2,1)S(1)}, u32[]{:S(2)}, u32[]{:S(2)}) collective-permute-start(bf16[4,24,768]{2,1,0:T(8,128)(2,1)S(1)} %slice.140), channel_id=1, source_target_pairs={{0,112},{16,0},{32,16},{48,32},{64,48},{80,64},{96,80},{112,96},{1... | collective-permute-start | bytes 442376 | tf_op jit(solution)/shard_map/ppermute | solution.py:36
  138.0 23.5 %collective-permute-start.22 = (bf16[512,768]{1,0:T(8,128)(2,1)S(1)}, bf16[512,768]{1,0:T(8,128)(2,1)S(1)}, u32[]{:S(2)}, u32[]{:S(2)}) collective-permute-start(bf16[512,768]{1,0:T(8,128)(2,1)S(1)} %fusion.10), channel_id=1, source_target_pairs={{0,8},{8,0},{1,9},{9,1},{2,10},{10,2},{3,11},{11,3},{4,12},{12,4},... | collective-permute-start | bytes 2359304 | tf_op jit(solution)/shard_map/ppermute | solution.py:36
  161.6 11.0 %collective-permute-start.23 = (bf16[256,768]{1,0:T(8,128)(2,1)S(1)}, bf16[256,768]{1,0:T(8,128)(2,1)S(1)}, u32[]{:S(2)}, u32[]{:S(2)}) collective-permute-start(bf16[256,768]{1,0:T(8,128)(2,1)S(1)} %fusion.15), channel_id=1, source_target_pairs={{0,128},{128,0},{1,129},{129,1},{2,130},{130,2},{3,131},{131,3},{4... | collective-permute-start | bytes 1179656 | tf_op jit(solution)/shard_map/ppermute | solution.py:36
  (25 other events, 286.7 us)

commit v3 on v2

--- a/solution.py
+++ b/solution.py
@@ -53,7 +53,7 @@
     return sum(t.astype(jnp.float32) for t in terms).astype(terms[0].dtype)
 
 
-def ring_scatter(part, far_up, far_down, axis, tie):
+def ring_scatter(part, far_up, far_down, axis):
     n = lax.axis_size(axis)
     h = n // 2
     cut = far_up.shape[2]
@@ -64,9 +64,7 @@
         up, down = shift(up, axis, 1), shift(down, axis, -1)
         if k > 1:
             up, down = add(up, part[k - 1]), add(down, part[n - k + 1])
-        if k == h - 1:
-            up, tie = lax.optimization_barrier((up, tie))
-    return add(part[0], up, down), tie
+    return add(part[0], up, down)
 
 
 def gradient_parts(order, tiles, outs, n_z):
@@ -133,8 +131,7 @@
     rel = jnp.arange(n_mp, dtype=jnp.int32)
     mp_of_rel = (rel // n_y ^ xl) * n_y + (rel % n_y + y) % n_y
 
-    states = jnp.concatenate([master[0], moment_one[0], moment_two[0]], axis=1).astype(bf16)
-    states = lax.all_to_all(states, DP, 0, 0, tiled=True)
+    w_in = lax.all_to_all(master[0].astype(bf16), DP, 0, 0, tiled=True)
 
     spot = jnp.arange(cols, dtype=jnp.int32)
     slab = spot // rows
@@ -160,14 +157,18 @@
         tiles += [[own], [down], far, [up]]
 
     w_at = (positions % per_row) * rows + positions // per_row
-    w_t = jnp.dot(one_hot(w_at, blocks), states[:, :width], preferred_element_type=f32).astype(bf16)
+    w_t = jnp.dot(one_hot(w_at, blocks), w_in, preferred_element_type=f32).astype(bf16)
     w_t = lax.all_to_all(w_t.reshape(n_mp, per_dev, rows, width), MP, 0, 0, tiled=True)
     w_t = w_t.transpose(0, 2, 1, 3).reshape(n_mp, rows, cols)
-    placed = jnp.dot(one_hot(positions, blocks), states, preferred_element_type=f32)
+    moments = jnp.concatenate([moment_one[0], moment_two[0]], axis=1).astype(bf16)
+    w_t, moments = lax.optimization_barrier((w_t, moments))
+    m_in = lax.all_to_all(moments, DP, 0, 0, tiled=True)
+    placed = one_hot(positions, blocks)
+    placed = jnp.dot(placed, jnp.concatenate([w_in, m_in], axis=1), preferred_element_type=f32)
     grads, far_up, far_down, ct_all = gradient_parts(mp_of_rel, tiles, [out_grad, og_x, og_c, og_xc], n_z)
     w_all = jnp.concatenate(ring_gather(w_t, "z")).reshape(n_z * n_mp * rows, cols)
 
-    grad, placed = ring_scatter(grads, far_up, far_down, "z", placed)
+    grad = ring_scatter(grads, far_up, far_down, "z")
     grad = lax.all_to_all(grad, MP, 0, 0, tiled=True)
     grad = grad.reshape(n_mp, rows, per_dev, width).transpose(1, 0, 2, 3).reshape(blocks, width).astype(f32)
 

time: 176 us -> 154 us (0.88)
  waiting for transfers between devices: 64.8 us -> 34 us
  blocking collectives: 11.5 us -> 0 us
  local copies, waits for them, and re-layouts: 3.09 us -> 13.5 us
  other arithmetic: 6.67 us -> 13.6 us
  starting transfers between devices: 67.7 us -> 70.3 us
    ppermute x32, waiting for transfers between devices: 61.4 us -> 25.1 us  [shift(): return lax.ppermute(a, axis, [(i, (i + by) % n) for i in range(n)])]
    all_to_all x1 -> x3, starting transfers between devices: 10.5 us -> 25.5 us  [the longest x1 12.4 us: local(): w_in = lax.all_to_all(master[0].astype(bf16), DP, 0, 0, tiled=True)]
    ppermute x32, starting transfers between devices: 53.8 us -> 40.5 us  [shift(): return lax.ppermute(a, axis, [(i, (i + by) % n) for i in range(n)])]
    all_to_all x1 -> x0, blocking collectives: 11.5 us -> none  [local(): grad = lax.all_to_all(grad, MP, 0, 0, tiled=True)]
    all_to_all x1 -> x3, waiting for transfers between devices: 0.01 us -> 8.91 us  [the longest x1 7.36 us: local(): w_in = lax.all_to_all(master[0].astype(bf16), DP, 0, 0, tiled=True)]
    convert_element_type x7, other arithmetic: 1.47 us -> 6.94 us  [add(): return sum((t.astype(jnp.float32) for t in terms)).astype(terms[0].dtype)]
    unnamed x38 -> x36, local copies, waits for them, and re-layouts: 0.33 us -> 4.34 us
    slice x4, local copies, waits for them, and re-layouts: 0.06 us -> 3.93 us  [local(): far = [shift(down[:cut], 'y', -1), shift(up[cut:], 'y', 1)]]
  transfers between devices with their start and end apart: 34 -> 36, of which waited for: 15 -> 10; matrix products, arithmetic and copies ran while one was open for 10% -> 22% of each run, Pallas kernels for 4% -> 5%
where the time goes in v3:
time: 154 us; the launch traced here: 152 us
  starting transfers between devices  70.3 us (46%)
  waiting for transfers between devices  34 us (22%)
  other arithmetic  13.6 us (9%)
  local copies, waits for them, and re-layouts  13.5 us (9%)
  matrix products  11.6 us (8%)
  Pallas kernels  7.55 us (5%)
  between operations  1.89 us (1%)
    ppermute x32, starting transfers between devices, shift(): return lax.ppermute(a, axis, [(i, (i + by) % n) for i in range(n)])  40.5 us
    ppermute x32, waiting for transfers between devices, shift(): return lax.ppermute(a, axis, [(i, (i + by) % n) for i in range(n)])  25.1 us
    all_to_all x1, starting transfers between devices, local(): w_in = lax.all_to_all(master[0].astype(bf16), DP, 0, 0, tiled=True)  12.4 us
    all_to_all x1, starting transfers between devices, local(): m_in = lax.all_to_all(moments, DP, 0, 0, tiled=True)  9.67 us
    pallas_call x1, Pallas kernels, gradient_parts(): pl.pallas_call(body, out_shape=(jax.ShapeDtypeStruct((n_z - 1, n_mp, rows...  7.55 us
    all_to_all x1, waiting for transfers between devices, local(): w_in = lax.all_to_all(master[0].astype(bf16), DP, 0, 0, tiled=True)  7.36 us
    convert_element_type x7, other arithmetic, add(): return sum((t.astype(jnp.float32) for t in terms)).astype(terms[0].dtype)  6.94 us
    unnamed x36, local copies, waits for them, and re-layouts  4.34 us
  transfers between devices with their start and end apart: 36, of which 10 were waited for; matrix products, arithmetic and copies ran while one was open for 22% of the time, Pallas kernels for 5%

profile of v3, /device:TPU:1, one launch (start us, length us, event | category | flops | bytes accessed | tf_op | source)
XLA Modules:
  0.0 152.5 jit_solution(221176766938469717)
XLA Ops:
  2.4 3.6 %collective-permute-start = (bf16[384,256]{1,0:T(8,128)(2,1)S(1)}, bf16[384,256]{1,0:T(8,128)(2,1)S(1)}, u32[]{:S(2)}, u32[]{:S(2)}) collective-permute-start(bf16[384,256]{1,0:T(8,128)(2,1)S(1)} %slice.125), channel_id=1, source_target_pairs={{0,128},{128,0},{1,129},{129,1},{2,130},{130,2},{3,131},{131,3},{4... | collective-permute-start | bytes 589832 | tf_op jit(solution)/shard_map/ppermute | solution.py:36
  7.0 12.4 %all-to-all-start = ((bf16[32,36,128]{2,1,0:T(8,128)(2,1)}), bf16[32,36,128]{2,1,0:T(8,128)(2,1)S(1)}, u32[]{:S(2)}, u32[]{:S(2)}) async-start(bf16[32,36,128]{2,1,0:T(8,128)(2,1)} %convert_element_type.130), calls=%async_computation | async-start | bytes 655360 | tf_op jit(solution)/shard_map/all_to_all | solution.py:134
  23.9 2.7 %collective-permute-start.2 = (bf16[192,1024]{1,0:T(8,128)(2,1)S(1)}, bf16[192,1024]{1,0:T(8,128)(2,1)S(1)}, u32[]{:S(2)}, u32[]{:S(2)}) collective-permute-start(bf16[192,1024]{1,0:T(8,128)(2,1)S(1)} %pad_maximum_fusion.1.refs_0_), channel_id=1, source_target_pairs={{0,3},{1,0},{2,1},{3,2},{4,7},{5,4},{6,5},{7,6},{8,11},{9,8},{10,9... | collective-permute-start | bytes 1179656 | tf_op jit(solution)/shard_map/ppermute | solution.py:36
  26.6 7.4 %all-to-all-done = bf16[32,36,128]{2,1,0:T(8,128)(2,1)S(1)} async-done(((bf16[32,36,128]{2,1,0:T(8,128)(2,1)}), bf16[32,36,128]{2,1,0:T(8,128)(2,1)S(1)}, u32[]{:S(2)}, u32[]{:S(2)}) %all-to-all-start) | async-done | bytes 294944 | tf_op jit(solution)/shard_map/all_to_all | solution.py:134
  35.8 4.2 %all-to-all-start.1 = ((bf16[8,6,24,128]{3,2,1,0:T(8,128)(2,1)}), bf16[8,6,24,128]{3,2,1,0:T(8,128)(2,1)S(1)}, u32[]{:S(2)}, u32[]{:S(2)}) async-start(bf16[8,6,24,128]{3,2,1,0:T(8,128)(2,1)} %bitcast.2), calls=%async_computation.1 | async-start | bytes 589824 | tf_op jit(solution)/shard_map/all_to_all | solution.py:161
  44.1 2.6 %collective-permute-start.12 = (bf16[256,768]{1,0:T(8,128)(2,1)}, bf16[256,768]{1,0:T(8,128)(2,1)S(1)}, u32[]{:S(2)}, u32[]{:S(2)}) collective-permute-start(bf16[256,768]{1,0:T(8,128)(2,1)} %refs_10_.1), channel_id=1, source_target_pairs={{0,8},{8,0},{1,9},{9,1},{2,10},{10,2},{3,11},{11,3},{4,12},{12,4},... | collective-permute-start | bytes 1179656 | tf_op jit(solution)/shard_map/ppermute | solution.py:36
  48.7 6.7 %collective-permute-done.9.refs_9_ = bf16[192,1024]{1,0:T(8,128)(2,1)} collective-permute-done((bf16[192,1024]{1,0:T(8,128)(2,1)}, bf16[192,1024]{1,0:T(8,128)(2,1)}, u32[]{:S(2)}, u32[]{:S(2)}) %collective-permute-start.9) | collective-permute-done | bytes 393248 | tf_op jit(solution)/shard_map/ppermute | solution.py:36
  60.9 2.6 %collective-permute-start.8 = (bf16[96,1024]{1,0:T(8,128)(2,1)}, bf16[96,1024]{1,0:T(8,128)(2,1)}, u32[]{:S(2)}, u32[]{:S(2)}) collective-permute-start(bf16[96,1024]{1,0:T(8,128)(2,1)} %slice.131), channel_id=1, source_target_pairs={{0,3},{1,0},{2,1},{3,2},{4,7},{5,4},{6,5},{7,6},{8,11},{9,8},{10,9... | collective-permute-start | bytes 589832 | tf_op jit(solution)/shard_map/ppermute | solution.py:36
  67.6 9.7 %all-to-all-start.2 = ((bf16[32,36,256]{2,1,0:T(8,128)(2,1)}), bf16[32,36,256]{2,1,0:T(8,128)(2,1)S(1)}, u32[]{:S(2)}, u32[]{:S(2)}) async-start(bf16[32,36,256]{2,1,0:T(8,128)(2,1)} %all_to_all.23), calls=%async_computation.2 | async-start | bytes 1310720 | tf_op jit(solution)/shard_map/all_to_all | solution.py:165
  77.3 7.5 %gradient_parts.1 = (bf16[7,8,24,768]{3,2,1,0:T(8,128)(2,1)}, bf16[8,24,384]{2,1,0:T(8,128)(2,1)}, bf16[8,24,384]{2,1,0:T(8,128)(2,1)}, bf16[8,8,24,1024]{3,2,1,0:T(8,128)(2,1)}) custom-call(s32[8]{0:T(128)} %fusion.55.order_ref, bf16[192,1024]{1,0:T(8,128)(2,1)} %copy-done.3, bf16[192,1024]{1,0:T(8,128)(2,1)} %copy-done.5, bf16[96,1024]{1,0:T(8,128)(2,1)} %copy-done.12, ...), custom_call_target="tpu_custom_call" | custom-call | tf_op jit(solution)/shard_map/gradient_parts/pallas_call | solution.py:104
  84.9 2.6 %collective-permute-start.28 = (bf16[8,24,384]{2,1,0:T(8,128)(2,1)}, bf16[8,24,384]{2,1,0:T(8,128)(2,1)S(1)}, u32[]{:S(2)}, u32[]{:S(2)}) collective-permute-start(bf16[8,24,384]{2,1,0:T(8,128)(2,1)} %get-tuple-element.15), channel_id=1, source_target_pairs={{0,112},{16,0},{32,16},{48,32},{64,48},{80,64},{96,80},{112,96},{1... | collective-permute-start | bytes 442376 | tf_op jit(solution)/shard_map/ppermute | solution.py:36
  88.7 2.7 %collective-permute-start.16 = (bf16[8,24,768]{2,1,0:T(8,128)(2,1)}, bf16[8,24,768]{2,1,0:T(8,128)(2,1)S(1)}, u32[]{:S(2)}, u32[]{:S(2)}) collective-permute-start(bf16[8,24,768]{2,1,0:T(8,128)(2,1)} %collective-permute-done.15), channel_id=1, source_target_pairs={{0,112},{16,0},{32,16},{48,32},{64,48},{80,64},{96,80},{112,96},{1... | collective-permute-start | bytes 884744 | tf_op jit(solution)/shard_map/ppermute | solution.py:36
  91.4 5.2 %collective-permute-done.28 = bf16[8,24,384]{2,1,0:T(8,128)(2,1)S(1)} collective-permute-done((bf16[8,24,384]{2,1,0:T(8,128)(2,1)}, bf16[8,24,384]{2,1,0:T(8,128)(2,1)S(1)}, u32[]{:S(2)}, u32[]{:S(2)}) %collective-permute-start.28) | collective-permute-done | bytes 147488 | tf_op jit(solution)/shard_map/ppermute | solution.py:36
  100.5 3.6 %collective-permute-done.19 = bf16[8,24,768]{2,1,0:T(8,128)(2,1)S(1)} collective-permute-done((bf16[8,24,768]{2,1,0:T(8,128)(2,1)}, bf16[8,24,768]{2,1,0:T(8,128)(2,1)S(1)}, u32[]{:S(2)}, u32[]{:S(2)}) %collective-permute-start.19) | collective-permute-done | bytes 294944 | tf_op jit(solution)/shard_map/ppermute | solution.py:36
  104.5 2.7 %collective-permute-start.21 = (bf16[4,24,768]{2,1,0:T(8,128)(2,1)S(1)}, bf16[4,24,768]{2,1,0:T(8,128)(2,1)S(1)}, u32[]{:S(2)}, u32[]{:S(2)}) collective-permute-start(bf16[4,24,768]{2,1,0:T(8,128)(2,1)S(1)} %slice.135), channel_id=1, source_target_pairs={{0,112},{16,0},{32,16},{48,32},{64,48},{80,64},{96,80},{112,96},{1... | collective-permute-start | bytes 442376 | tf_op jit(solution)/shard_map/ppermute | solution.py:36
  110.7 2.7 %collective-permute-start.30 = (bf16[8,24,768]{2,1,0:T(8,128)(2,1)S(1)}, bf16[8,24,768]{2,1,0:T(8,128)(2,1)S(1)}, u32[]{:S(2)}, u32[]{:S(2)}) collective-permute-start(bf16[8,24,768]{2,1,0:T(8,128)(2,1)S(1)} %get-tuple-element.22), channel_id=1, source_target_pairs={{0,112},{16,0},{32,16},{48,32},{64,48},{80,64},{96,80},{112,96},{1... | collective-permute-start | bytes 884744 | tf_op jit(solution)/shard_map/ppermute | solution.py:36
  115.7 2.4 %fusion.10 = bf16[512,768]{1,0:T(8,128)(2,1)} fusion(bf16[1536,768]{1,0:T(8,128)(2,1)S(1)} %bitcast.45, bf16[1536,1024]{1,0:T(8,128)(2,1)S(1)} %bitcast.47), kind=kOutput, calls=%fused_computation.13 | convolution fusion | flops 1208352768 | bytes 4718592 | tf_op jit(solution)/shard_map/dot_general | solution.py:176
  121.2 2.4 %collective-permute-start.31 = (bf16[8,24,768]{2,1,0:T(8,128)(2,1)}, bf16[8,24,768]{2,1,0:T(8,128)(2,1)}, u32[]{:S(2)}, u32[]{:S(2)}) collective-permute-start(bf16[8,24,768]{2,1,0:T(8,128)(2,1)} %get-tuple-element.20), channel_id=1, source_target_pairs={{0,112},{16,0},{32,16},{48,32},{64,48},{80,64},{96,80},{112,96},{1... | collective-permute-start | bytes 884744 | tf_op jit(solution)/shard_map/ppermute | solution.py:36
  123.6 3.1 %fusion.6 = f32[512,768]{1,0:T(8,128)S(1)} fusion(bf16[1536,768]{1,0:T(8,128)(2,1)} %bitcast.46, bf16[1536,1024]{1,0:T(8,128)(2,1)S(1)} %bitcast.48), kind=kOutput, calls=%fused_computation.9 | convolution fusion | flops 1207959552 | bytes 5505024 | tf_op jit(solution)/shard_map/dot_general | solution.py:178
  126.9 3.8 %fusion.1 = f32[1152,384]{1,0:T(8,128)} fusion(s32[1152]{0:T(1024)S(1)} %sub.54, bf16[1152,256]{1,0:T(8,128)(2,1)S(1)} %all_to_all.25, bf16[1152,128]{1,0:T(8,128)(2,1)} %copy-done.11), kind=kOutput, calls=%fused_computation.3 | convolution fusion | flops 1022312448 | bytes 2658816 | tf_op jit(solution)/shard_map/dot_general | solution.py:167
  132.6 3.4 %all-to-all-start.3 = ((bf16[8,24,768]{2,1,0:T(8,128)(2,1)}), bf16[8,24,768]{2,1,0:T(8,128)(2,1)S(1)}, u32[]{:S(2)}, u32[]{:S(2)}) async-start(bf16[8,24,768]{2,1,0:T(8,128)(2,1)} %fusion.28), calls=%async_computation.3 | async-start | bytes 589824 | tf_op jit(solution)/shard_map/all_to_all | solution.py:172
  137.9 2.8 %collective-permute-start.23 = (bf16[256,768]{1,0:T(8,128)(2,1)}, bf16[256,768]{1,0:T(8,128)(2,1)}, u32[]{:S(2)}, u32[]{:S(2)}) collective-permute-start(bf16[256,768]{1,0:T(8,128)(2,1)} %fusion.18), channel_id=1, source_target_pairs={{0,128},{128,0},{1,129},{129,1},{2,130},{130,2},{3,131},{131,3},{4... | collective-permute-start | bytes 1179656 | tf_op jit(solution)/shard_map/ppermute | solution.py:36
  142.7 2.9 %fusion.30 = (f32[1,1152,128]{2,1,0:T(8,128)}, f32[1,1152,128]{2,1,0:T(8,128)}, f32[1,1152,128]{2,1,0:T(8,128)}) fusion(f32[1152,128]{1,0:T(8,128)S(1)} %reshape.170, f32[1152,384]{1,0:T(8,128)} %fusion.1), kind=kLoop, calls=%fused_computation.54 | loop fusion | flops 2211840 | bytes 4128768 | tf_op jit(solution)/shard_map/broadcast_in_dim | solution.py:185
  145.6 4.9 %collective-permute-done.23 = bf16[256,768]{1,0:T(8,128)(2,1)} collective-permute-done((bf16[256,768]{1,0:T(8,128)(2,1)}, bf16[256,768]{1,0:T(8,128)(2,1)}, u32[]{:S(2)}, u32[]{:S(2)}) %collective-permute-start.23) | collective-permute-done | bytes 393248 | tf_op jit(solution)/shard_map/ppermute | solution.py:36
  (134 shorter events, 45.7 us)
Async XLA Ops:
  2.4 19.4 %collective-permute-start = (bf16[384,256]{1,0:T(8,128)(2,1)S(1)}, bf16[384,256]{1,0:T(8,128)(2,1)S(1)}, u32[]{:S(2)}, u32[]{:S(2)}) collective-permute-start(bf16[384,256]{1,0:T(8,128)(2,1)S(1)} %slice.125), channel_id=1, source_target_pairs={{0,128},{128,0},{1,129},{129,1},{2,130},{130,2},{3,131},{131,3},{4... | collective-permute-start | bytes 589832 | tf_op jit(solution)/shard_map/ppermute | solution.py:36
  6.1 38.0 %collective-permute-start.11 = (bf16[256,768]{1,0:T(8,128)(2,1)}, bf16[256,768]{1,0:T(8,128)(2,1)}, u32[]{:S(2)}, u32[]{:S(2)}) collective-permute-start(bf16[256,768]{1,0:T(8,128)(2,1)} %refs_10_.1), channel_id=1, source_target_pairs={{0,128},{128,0},{1,129},{129,1},{2,130},{130,2},{3,131},{131,3},{4... | collective-permute-start | bytes 1179656 | tf_op jit(solution)/shard_map/ppermute | solution.py:36
  7.0 27.0 %all-to-all-start = ((bf16[32,36,128]{2,1,0:T(8,128)(2,1)}), bf16[32,36,128]{2,1,0:T(8,128)(2,1)S(1)}, u32[]{:S(2)}, u32[]{:S(2)}) async-start(bf16[32,36,128]{2,1,0:T(8,128)(2,1)} %convert_element_type.130), calls=%async_computation | async-start | bytes 655360 | tf_op jit(solution)/shard_map/all_to_all | solution.py:134
  23.4 17.7 %collective-permute-start.6 = (bf16[192,1024]{1,0:T(8,128)(2,1)S(1)}, bf16[192,1024]{1,0:T(8,128)(2,1)}, u32[]{:S(2)}, u32[]{:S(2)}) collective-permute-start(bf16[192,1024]{1,0:T(8,128)(2,1)S(1)} %pad_maximum_fusion.1.refs_0_), channel_id=1, source_target_pairs={{0,4},{4,0},{1,5},{5,1},{2,6},{6,2},{3,7},{7,3},{8,12},{12,8},{9,1... | collective-permute-start | bytes 1179656 | tf_op jit(solution)/shard_map/ppermute | solution.py:36
  23.9 22.9 %collective-permute-start.2 = (bf16[192,1024]{1,0:T(8,128)(2,1)S(1)}, bf16[192,1024]{1,0:T(8,128)(2,1)S(1)}, u32[]{:S(2)}, u32[]{:S(2)}) collective-permute-start(bf16[192,1024]{1,0:T(8,128)(2,1)S(1)} %pad_maximum_fusion.1.refs_0_), channel_id=1, source_target_pairs={{0,3},{1,0},{2,1},{3,2},{4,7},{5,4},{6,5},{7,6},{8,11},{9,8},{10,9... | collective-permute-start | bytes 1179656 | tf_op jit(solution)/shard_map/ppermute | solution.py:36
  26.6 20.3 %collective-permute-start.4 = (bf16[192,1024]{1,0:T(8,128)(2,1)S(1)}, bf16[192,1024]{1,0:T(8,128)(2,1)S(1)}, u32[]{:S(2)}, u32[]{:S(2)}) collective-permute-start(bf16[192,1024]{1,0:T(8,128)(2,1)S(1)} %pad_maximum_fusion.1.refs_0_), channel_id=1, source_target_pairs={{0,1},{1,2},{2,3},{3,0},{4,5},{5,6},{6,7},{7,4},{8,9},{9,10},{10,1... | collective-permute-start | bytes 1179656 | tf_op jit(solution)/shard_map/ppermute | solution.py:36
  35.8 12.9 %all-to-all-start.1 = ((bf16[8,6,24,128]{3,2,1,0:T(8,128)(2,1)}), bf16[8,6,24,128]{3,2,1,0:T(8,128)(2,1)S(1)}, u32[]{:S(2)}, u32[]{:S(2)}) async-start(bf16[8,6,24,128]{3,2,1,0:T(8,128)(2,1)} %bitcast.2), calls=%async_computation.1 | async-start | bytes 589824 | tf_op jit(solution)/shard_map/all_to_all | solution.py:161
  41.2 14.2 %collective-permute-start.9 = (bf16[192,1024]{1,0:T(8,128)(2,1)}, bf16[192,1024]{1,0:T(8,128)(2,1)}, u32[]{:S(2)}, u32[]{:S(2)}) collective-permute-start(bf16[192,1024]{1,0:T(8,128)(2,1)} %collective-permute-done.6.refs_5_), channel_id=1, source_target_pairs={{0,1},{1,2},{2,3},{3,0},{4,5},{5,6},{6,7},{7,4},{8,9},{9,10},{10,1... | collective-permute-start | bytes 1179656 | tf_op jit(solution)/shard_map/ppermute | solution.py:36
  42.7 12.7 %collective-permute-start.7 = (bf16[192,1024]{1,0:T(8,128)(2,1)}, bf16[192,1024]{1,0:T(8,128)(2,1)}, u32[]{:S(2)}, u32[]{:S(2)}) collective-permute-start(bf16[192,1024]{1,0:T(8,128)(2,1)} %collective-permute-done.6.refs_5_), channel_id=1, source_target_pairs={{0,3},{1,0},{2,1},{3,2},{4,7},{5,4},{6,5},{7,6},{8,11},{9,8},{10,9... | collective-permute-start | bytes 1179656 | tf_op jit(solution)/shard_map/ppermute | solution.py:36
  44.1 16.7 %collective-permute-start.12 = (bf16[256,768]{1,0:T(8,128)(2,1)}, bf16[256,768]{1,0:T(8,128)(2,1)S(1)}, u32[]{:S(2)}, u32[]{:S(2)}) collective-permute-start(bf16[256,768]{1,0:T(8,128)(2,1)} %refs_10_.1), channel_id=1, source_target_pairs={{0,8},{8,0},{1,9},{9,1},{2,10},{10,2},{3,11},{11,3},{4,12},{12,4},... | collective-permute-start | bytes 1179656 | tf_op jit(solution)/shard_map/ppermute | solution.py:36
  46.7 14.1 %collective-permute-start.13 = (bf16[256,768]{1,0:T(8,128)(2,1)}, bf16[256,768]{1,0:T(8,128)(2,1)}, u32[]{:S(2)}, u32[]{:S(2)}) collective-permute-start(bf16[256,768]{1,0:T(8,128)(2,1)} %collective-permute-done.11.refs_11_), channel_id=1, source_target_pairs={{0,8},{8,0},{1,9},{9,1},{2,10},{10,2},{3,11},{11,3},{4,12},{12,4},... | collective-permute-start | bytes 1179656 | tf_op jit(solution)/shard_map/ppermute | solution.py:36
  46.9 14.0 %collective-permute-start.3 = (bf16[96,1024]{1,0:T(8,128)(2,1)S(1)}, bf16[96,1024]{1,0:T(8,128)(2,1)S(1)}, u32[]{:S(2)}, u32[]{:S(2)}) collective-permute-start(bf16[96,1024]{1,0:T(8,128)(2,1)S(1)} %slice.129), channel_id=1, source_target_pairs={{0,3},{1,0},{2,1},{3,2},{4,7},{5,4},{6,5},{7,6},{8,11},{9,8},{10,9... | collective-permute-start | bytes 589832 | tf_op jit(solution)/shard_map/ppermute | solution.py:36
  60.8 16.5 %collective-permute-start.5 = (bf16[96,1024]{1,0:T(8,128)(2,1)}, bf16[96,1024]{1,0:T(8,128)(2,1)}, u32[]{:S(2)}, u32[]{:S(2)}) collective-permute-start(bf16[96,1024]{1,0:T(8,128)(2,1)} %slice.130), channel_id=1, source_target_pairs={{0,1},{1,2},{2,3},{3,0},{4,5},{5,6},{6,7},{7,4},{8,9},{9,10},{10,1... | collective-permute-start | bytes 589832 | tf_op jit(solution)/shard_map/ppermute | solution.py:36
  60.8 16.5 %collective-permute-start.10 = (bf16[96,1024]{1,0:T(8,128)(2,1)}, bf16[96,1024]{1,0:T(8,128)(2,1)}, u32[]{:S(2)}, u32[]{:S(2)}) collective-permute-start(bf16[96,1024]{1,0:T(8,128)(2,1)} %slice.132), channel_id=1, source_target_pairs={{0,1},{1,2},{2,3},{3,0},{4,5},{5,6},{6,7},{7,4},{8,9},{9,10},{10,1... | collective-permute-start | bytes 589832 | tf_op jit(solution)/shard_map/ppermute | solution.py:36
  60.9 16.4 %collective-permute-start.8 = (bf16[96,1024]{1,0:T(8,128)(2,1)}, bf16[96,1024]{1,0:T(8,128)(2,1)}, u32[]{:S(2)}, u32[]{:S(2)}) collective-permute-start(bf16[96,1024]{1,0:T(8,128)(2,1)} %slice.131), channel_id=1, source_target_pairs={{0,3},{1,0},{2,1},{3,2},{4,7},{5,4},{6,5},{7,6},{8,11},{9,8},{10,9... | collective-permute-start | bytes 589832 | tf_op jit(solution)/shard_map/ppermute | solution.py:36
  64.1 24.6 %collective-permute-start.15 = (bf16[8,24,768]{2,1,0:T(8,128)(2,1)}, bf16[8,24,768]{2,1,0:T(8,128)(2,1)}, u32[]{:S(2)}, u32[]{:S(2)}) collective-permute-start(bf16[8,24,768]{2,1,0:T(8,128)(2,1)} %collective-permute-done.14), channel_id=1, source_target_pairs={{0,112},{16,0},{32,16},{48,32},{64,48},{80,64},{96,80},{112,96},{1... | collective-permute-start | bytes 884744 | tf_op jit(solution)/shard_map/ppermute | solution.py:36
  65.4 26.1 %collective-permute-start.18 = (bf16[8,24,768]{2,1,0:T(8,128)(2,1)}, bf16[8,24,768]{2,1,0:T(8,128)(2,1)}, u32[]{:S(2)}, u32[]{:S(2)}) collective-permute-start(bf16[8,24,768]{2,1,0:T(8,128)(2,1)} %collective-permute-done.17), channel_id=1, source_target_pairs={{0,16},{16,32},{32,48},{48,64},{64,80},{80,96},{96,112},{112,0},{1... | collective-permute-start | bytes 884744 | tf_op jit(solution)/shard_map/ppermute | solution.py:36
  67.6 59.1 %all-to-all-start.2 = ((bf16[32,36,256]{2,1,0:T(8,128)(2,1)}), bf16[32,36,256]{2,1,0:T(8,128)(2,1)S(1)}, u32[]{:S(2)}, u32[]{:S(2)}) async-start(bf16[32,36,256]{2,1,0:T(8,128)(2,1)} %all_to_all.23), calls=%async_computation.2 | async-start | bytes 1310720 | tf_op jit(solution)/shard_map/all_to_all | solution.py:165
  88.7 15.8 %collective-permute-start.16 = (bf16[8,24,768]{2,1,0:T(8,128)(2,1)}, bf16[8,24,768]{2,1,0:T(8,128)(2,1)S(1)}, u32[]{:S(2)}, u32[]{:S(2)}) collective-permute-start(bf16[8,24,768]{2,1,0:T(8,128)(2,1)} %collective-permute-done.15), channel_id=1, source_target_pairs={{0,112},{16,0},{32,16},{48,32},{64,48},{80,64},{96,80},{112,96},{1... | collective-permute-start | bytes 884744 | tf_op jit(solution)/shard_map/ppermute | solution.py:36
  91.4 12.7 %collective-permute-start.19 = (bf16[8,24,768]{2,1,0:T(8,128)(2,1)}, bf16[8,24,768]{2,1,0:T(8,128)(2,1)S(1)}, u32[]{:S(2)}, u32[]{:S(2)}) collective-permute-start(bf16[8,24,768]{2,1,0:T(8,128)(2,1)} %collective-permute-done.18), channel_id=1, source_target_pairs={{0,16},{16,32},{32,48},{48,64},{64,80},{80,96},{96,112},{112,0},{1... | collective-permute-start | bytes 884744 | tf_op jit(solution)/shard_map/ppermute | solution.py:36
  96.7 12.6 %collective-permute-start.29 = (bf16[8,24,768]{2,1,0:T(8,128)(2,1)S(1)}, bf16[8,24,768]{2,1,0:T(8,128)(2,1)S(1)}, u32[]{:S(2)}, u32[]{:S(2)}) collective-permute-start(bf16[8,24,768]{2,1,0:T(8,128)(2,1)S(1)} %pad_maximum_fusion.3), channel_id=1, source_target_pairs={{0,112},{16,0},{32,16},{48,32},{64,48},{80,64},{96,80},{112,96},{1... | collective-permute-start | bytes 884744 | tf_op jit(solution)/shard_map/ppermute | solution.py:36
  98.5 12.0 %collective-permute-start.25 = (bf16[8,24,768]{2,1,0:T(8,128)(2,1)S(1)}, bf16[8,24,768]{2,1,0:T(8,128)(2,1)S(1)}, u32[]{:S(2)}, u32[]{:S(2)}) collective-permute-start(bf16[8,24,768]{2,1,0:T(8,128)(2,1)S(1)} %pad_maximum_fusion.2), channel_id=1, source_target_pairs={{0,16},{16,32},{32,48},{48,64},{64,80},{80,96},{96,112},{112,0},{1... | collective-permute-start | bytes 884744 | tf_op jit(solution)/shard_map/ppermute | solution.py:36
  118.1 18.0 %collective-permute-start.22 = (bf16[512,768]{1,0:T(8,128)(2,1)}, bf16[512,768]{1,0:T(8,128)(2,1)}, u32[]{:S(2)}, u32[]{:S(2)}) collective-permute-start(bf16[512,768]{1,0:T(8,128)(2,1)} %fusion.10), channel_id=1, source_target_pairs={{0,8},{8,0},{1,9},{9,1},{2,10},{10,2},{3,11},{11,3},{4,12},{12,4},... | collective-permute-start | bytes 2359304 | tf_op jit(solution)/shard_map/ppermute | solution.py:36
  137.9 12.6 %collective-permute-start.23 = (bf16[256,768]{1,0:T(8,128)(2,1)}, bf16[256,768]{1,0:T(8,128)(2,1)}, u32[]{:S(2)}, u32[]{:S(2)}) collective-permute-start(bf16[256,768]{1,0:T(8,128)(2,1)} %fusion.18), channel_id=1, source_target_pairs={{0,128},{128,0},{1,129},{129,1},{2,130},{130,2},{3,131},{131,3},{4... | collective-permute-start | bytes 1179656 | tf_op jit(solution)/shard_map/ppermute | solution.py:36
  (26 other events, 268.9 us)

commit v4 on v3

--- a/solution.py
+++ b/solution.py
@@ -79,26 +79,29 @@
 
     def body(order_ref, *refs):
         tile_refs, o_refs = list(refs[: len(flat)]), refs[len(flat) : len(flat) + len(outs)]
-        g_ref, up_ref, down_ref, t_ref = refs[len(flat) + len(outs) :]
+        g_ref, up_ref, down_ref, t_ref, o_all, t_all = refs[len(flat) + len(outs) :]
         step = width // len(outs)
-        for i in range(n_mp):
-            at = order_ref[i]
-            k = 0
-            for ref in [tile_refs.pop(0) for _ in range(sizes[i])]:
-                acc = None
-                for j, o_ref in enumerate(o_refs):
-                    term = jnp.dot(ref[:, j * step : (j + 1) * step], o_ref[...], preferred_element_type=jnp.float32)
-                    acc = term if acc is None else acc + term
-                acc = acc.astype(kind)
-                for r in range(0, ref.shape[0], rows):
-                    piece = acc[r : r + rows]
+        for j, o_ref in enumerate(o_refs):
+            o_all[j * step : (j + 1) * step] = o_ref[...]
+        depth = n_z * rows
+        at = 0
+        for ref in tile_refs:
+            t_all[at : at + ref.shape[0]] = ref[...]
+            at += ref.shape[0]
+        for side in range(2):
+            lanes = slice(side * cols // 2, (side + 1) * cols // 2)
+            acc = jnp.dot(t_all[...], o_all[:, lanes], preferred_element_type=jnp.float32)
+            for i in range(n_mp):
+                to = order_ref[i]
+                for k in range(n_z):
+                    at = i * depth + k * rows
+                    piece = acc[at : at + rows].astype(kind)
                     if k == far:
-                        up_ref[at] = piece[:, : cols // 2]
-                        down_ref[at] = piece[:, cols // 2 :]
+                        (down_ref if side else up_ref)[to] = piece
                     else:
-                        g_ref[k - (k > far), at] = piece
-                    t_ref[k, at] = ref[r : r + rows]
-                    k += 1
+                        g_ref[k - (k > far), to, :, lanes] = piece
+                    if side == 0:
+                        t_ref[k, to] = t_all[at : at + rows]
 
     vmem = pl.BlockSpec(memory_space=pltpu.VMEM)
     g, up, down, tiles_all = pl.pallas_call(
@@ -111,6 +114,7 @@
         ),
         in_specs=[pl.BlockSpec(memory_space=pltpu.SMEM)] + [vmem] * (len(flat) + len(outs)),
         out_specs=(vmem,) * 4,
+        scratch_shapes=[pltpu.VMEM((width, cols), kind), pltpu.VMEM((n_mp * n_z * rows, width), kind)],
         name="gradient_parts",
     )(order, *flat, *outs)
     return {k: g[k - (k > far)] for k in range(n_z) if k != far}, up, down, tiles_all

time: 154 us -> 154 us (level)
  no operation moved by 1% of the time
where the time goes in v4:
time: 154 us; the launch traced here: 152 us
  starting transfers between devices  70.3 us (46%)
  waiting for transfers between devices  33.4 us (22%)
  other arithmetic  13.6 us (9%)
  local copies, waits for them, and re-layouts  13.5 us (9%)
  matrix products  11.6 us (8%)
  Pallas kernels  8.12 us (5%)
  between operations  1.89 us (1%)
    ppermute x32, starting transfers between devices, shift(): return lax.ppermute(a, axis, [(i, (i + by) % n) for i in range(n)])  40.6 us
    ppermute x32, waiting for transfers between devices, shift(): return lax.ppermute(a, axis, [(i, (i + by) % n) for i in range(n)])  24.5 us
    all_to_all x1, starting transfers between devices, local(): w_in = lax.all_to_all(master[0].astype(bf16), DP, 0, 0, tiled=True)  12.4 us
    all_to_all x1, starting transfers between devices, local(): m_in = lax.all_to_all(moments, DP, 0, 0, tiled=True)  9.67 us
    pallas_call x1, Pallas kernels, gradient_parts(): pl.pallas_call(body, out_shape=(jax.ShapeDtypeStruct((n_z - 1, n_mp, rows...  8.12 us
    all_to_all x1, waiting for transfers between devices, local(): w_in = lax.all_to_all(master[0].astype(bf16), DP, 0, 0, tiled=True)  7.36 us
    convert_element_type x7, other arithmetic, add(): return sum((t.astype(jnp.float32) for t in terms)).astype(terms[0].dtype)  6.94 us
    unnamed x36, local copies, waits for them, and re-layouts  4.34 us
  transfers between devices with their start and end apart: 36, of which 10 were waited for; matrix products, arithmetic and copies ran while one was open for 22% of the time, Pallas kernels for 5%

profile of v4, /device:TPU:1, one launch (start us, length us, event | category | flops | bytes accessed | tf_op | source)
XLA Modules:
  0.0 152.5 jit_solution(326376749705601458)
XLA Ops:
  2.4 3.6 %collective-permute-start = (bf16[384,256]{1,0:T(8,128)(2,1)S(1)}, bf16[384,256]{1,0:T(8,128)(2,1)S(1)}, u32[]{:S(2)}, u32[]{:S(2)}) collective-permute-start(bf16[384,256]{1,0:T(8,128)(2,1)S(1)} %slice.125), channel_id=1, source_target_pairs={{0,128},{128,0},{1,129},{129,1},{2,130},{130,2},{3,131},{131,3},{4... | collective-permute-start | bytes 589832 | tf_op jit(solution)/shard_map/ppermute | solution.py:36
  7.0 12.4 %all-to-all-start = ((bf16[32,36,128]{2,1,0:T(8,128)(2,1)}), bf16[32,36,128]{2,1,0:T(8,128)(2,1)S(1)}, u32[]{:S(2)}, u32[]{:S(2)}) async-start(bf16[32,36,128]{2,1,0:T(8,128)(2,1)} %convert_element_type.130), calls=%async_computation | async-start | bytes 655360 | tf_op jit(solution)/shard_map/all_to_all | solution.py:138
  23.9 2.7 %collective-permute-start.2 = (bf16[192,1024]{1,0:T(8,128)(2,1)S(1)}, bf16[192,1024]{1,0:T(8,128)(2,1)S(1)}, u32[]{:S(2)}, u32[]{:S(2)}) collective-permute-start(bf16[192,1024]{1,0:T(8,128)(2,1)S(1)} %pad_maximum_fusion.1.refs_0_), channel_id=1, source_target_pairs={{0,3},{1,0},{2,1},{3,2},{4,7},{5,4},{6,5},{7,6},{8,11},{9,8},{10,9... | collective-permute-start | bytes 1179656 | tf_op jit(solution)/shard_map/ppermute | solution.py:36
  26.6 7.4 %all-to-all-done = bf16[32,36,128]{2,1,0:T(8,128)(2,1)S(1)} async-done(((bf16[32,36,128]{2,1,0:T(8,128)(2,1)}), bf16[32,36,128]{2,1,0:T(8,128)(2,1)S(1)}, u32[]{:S(2)}, u32[]{:S(2)}) %all-to-all-start) | async-done | bytes 294944 | tf_op jit(solution)/shard_map/all_to_all | solution.py:138
  35.8 4.2 %all-to-all-start.1 = ((bf16[8,6,24,128]{3,2,1,0:T(8,128)(2,1)}), bf16[8,6,24,128]{3,2,1,0:T(8,128)(2,1)S(1)}, u32[]{:S(2)}, u32[]{:S(2)}) async-start(bf16[8,6,24,128]{3,2,1,0:T(8,128)(2,1)} %bitcast.2), calls=%async_computation.1 | async-start | bytes 589824 | tf_op jit(solution)/shard_map/all_to_all | solution.py:165
  44.1 2.6 %collective-permute-start.12 = (bf16[256,768]{1,0:T(8,128)(2,1)}, bf16[256,768]{1,0:T(8,128)(2,1)S(1)}, u32[]{:S(2)}, u32[]{:S(2)}) collective-permute-start(bf16[256,768]{1,0:T(8,128)(2,1)} %refs_10_.1), channel_id=1, source_target_pairs={{0,8},{8,0},{1,9},{9,1},{2,10},{10,2},{3,11},{11,3},{4,12},{12,4},... | collective-permute-start | bytes 1179656 | tf_op jit(solution)/shard_map/ppermute | solution.py:36
  48.7 6.7 %collective-permute-done.9.refs_9_ = bf16[192,1024]{1,0:T(8,128)(2,1)} collective-permute-done((bf16[192,1024]{1,0:T(8,128)(2,1)}, bf16[192,1024]{1,0:T(8,128)(2,1)}, u32[]{:S(2)}, u32[]{:S(2)}) %collective-permute-start.9) | collective-permute-done | bytes 393248 | tf_op jit(solution)/shard_map/ppermute | solution.py:36
  60.9 2.6 %collective-permute-start.8 = (bf16[96,1024]{1,0:T(8,128)(2,1)}, bf16[96,1024]{1,0:T(8,128)(2,1)}, u32[]{:S(2)}, u32[]{:S(2)}) collective-permute-start(bf16[96,1024]{1,0:T(8,128)(2,1)} %slice.131), channel_id=1, source_target_pairs={{0,3},{1,0},{2,1},{3,2},{4,7},{5,4},{6,5},{7,6},{8,11},{9,8},{10,9... | collective-permute-start | bytes 589832 | tf_op jit(solution)/shard_map/ppermute | solution.py:36
  67.6 9.7 %all-to-all-start.2 = ((bf16[32,36,256]{2,1,0:T(8,128)(2,1)}), bf16[32,36,256]{2,1,0:T(8,128)(2,1)S(1)}, u32[]{:S(2)}, u32[]{:S(2)}) async-start(bf16[32,36,256]{2,1,0:T(8,128)(2,1)} %all_to_all.23), calls=%async_computation.2 | async-start | bytes 1310720 | tf_op jit(solution)/shard_map/all_to_all | solution.py:169
  77.3 8.1 %gradient_parts.1 = (bf16[7,8,24,768]{3,2,1,0:T(8,128)(2,1)}, bf16[8,24,384]{2,1,0:T(8,128)(2,1)}, bf16[8,24,384]{2,1,0:T(8,128)(2,1)}, bf16[8,8,24,1024]{3,2,1,0:T(8,128)(2,1)}) custom-call(s32[8]{0:T(128)} %fusion.55.order_ref, bf16[192,1024]{1,0:T(8,128)(2,1)} %copy-done.3, bf16[192,1024]{1,0:T(8,128)(2,1)} %copy-done.5, bf16[96,1024]{1,0:T(8,128)(2,1)} %copy-done.12, ...), custom_call_target="tpu_custom_call" | custom-call | tf_op jit(solution)/shard_map/gradient_parts/pallas_call | solution.py:107
  85.5 2.6 %collective-permute-start.28 = (bf16[8,24,384]{2,1,0:T(8,128)(2,1)}, bf16[8,24,384]{2,1,0:T(8,128)(2,1)S(1)}, u32[]{:S(2)}, u32[]{:S(2)}) collective-permute-start(bf16[8,24,384]{2,1,0:T(8,128)(2,1)} %get-tuple-element.15), channel_id=1, source_target_pairs={{0,112},{16,0},{32,16},{48,32},{64,48},{80,64},{96,80},{112,96},{1... | collective-permute-start | bytes 442376 | tf_op jit(solution)/shard_map/ppermute | solution.py:36
  89.3 2.7 %collective-permute-start.16 = (bf16[8,24,768]{2,1,0:T(8,128)(2,1)}, bf16[8,24,768]{2,1,0:T(8,128)(2,1)S(1)}, u32[]{:S(2)}, u32[]{:S(2)}) collective-permute-start(bf16[8,24,768]{2,1,0:T(8,128)(2,1)} %collective-permute-done.15), channel_id=1, source_target_pairs={{0,112},{16,0},{32,16},{48,32},{64,48},{80,64},{96,80},{112,96},{1... | collective-permute-start | bytes 884744 | tf_op jit(solution)/shard_map/ppermute | solution.py:36
  92.1 4.5 %collective-permute-done.28 = bf16[8,24,384]{2,1,0:T(8,128)(2,1)S(1)} collective-permute-done((bf16[8,24,384]{2,1,0:T(8,128)(2,1)}, bf16[8,24,384]{2,1,0:T(8,128)(2,1)S(1)}, u32[]{:S(2)}, u32[]{:S(2)}) %collective-permute-start.28) | collective-permute-done | bytes 147488 | tf_op jit(solution)/shard_map/ppermute | solution.py:36
  100.5 3.6 %collective-permute-done.19 = bf16[8,24,768]{2,1,0:T(8,128)(2,1)S(1)} collective-permute-done((bf16[8,24,768]{2,1,0:T(8,128)(2,1)}, bf16[8,24,768]{2,1,0:T(8,128)(2,1)S(1)}, u32[]{:S(2)}, u32[]{:S(2)}) %collective-permute-start.19) | collective-permute-done | bytes 294944 | tf_op jit(solution)/shard_map/ppermute | solution.py:36
  104.5 2.7 %collective-permute-start.21 = (bf16[4,24,768]{2,1,0:T(8,128)(2,1)S(1)}, bf16[4,24,768]{2,1,0:T(8,128)(2,1)S(1)}, u32[]{:S(2)}, u32[]{:S(2)}) collective-permute-start(bf16[4,24,768]{2,1,0:T(8,128)(2,1)S(1)} %slice.135), channel_id=1, source_target_pairs={{0,112},{16,0},{32,16},{48,32},{64,48},{80,64},{96,80},{112,96},{1... | collective-permute-start | bytes 442376 | tf_op jit(solution)/shard_map/ppermute | solution.py:36
  110.7 2.7 %collective-permute-start.30 = (bf16[8,24,768]{2,1,0:T(8,128)(2,1)S(1)}, bf16[8,24,768]{2,1,0:T(8,128)(2,1)S(1)}, u32[]{:S(2)}, u32[]{:S(2)}) collective-permute-start(bf16[8,24,768]{2,1,0:T(8,128)(2,1)S(1)} %get-tuple-element.22), channel_id=1, source_target_pairs={{0,112},{16,0},{32,16},{48,32},{64,48},{80,64},{96,80},{112,96},{1... | collective-permute-start | bytes 884744 | tf_op jit(solution)/shard_map/ppermute | solution.py:36
  115.7 2.4 %fusion.10 = bf16[512,768]{1,0:T(8,128)(2,1)} fusion(bf16[1536,768]{1,0:T(8,128)(2,1)S(1)} %bitcast.45, bf16[1536,1024]{1,0:T(8,128)(2,1)S(1)} %bitcast.47), kind=kOutput, calls=%fused_computation.13 | convolution fusion | flops 1208352768 | bytes 4718592 | tf_op jit(solution)/shard_map/dot_general | solution.py:180
  121.2 2.4 %collective-permute-start.31 = (bf16[8,24,768]{2,1,0:T(8,128)(2,1)}, bf16[8,24,768]{2,1,0:T(8,128)(2,1)}, u32[]{:S(2)}, u32[]{:S(2)}) collective-permute-start(bf16[8,24,768]{2,1,0:T(8,128)(2,1)} %get-tuple-element.20), channel_id=1, source_target_pairs={{0,112},{16,0},{32,16},{48,32},{64,48},{80,64},{96,80},{112,96},{1... | collective-permute-start | bytes 884744 | tf_op jit(solution)/shard_map/ppermute | solution.py:36
  123.6 3.1 %fusion.6 = f32[512,768]{1,0:T(8,128)S(1)} fusion(bf16[1536,768]{1,0:T(8,128)(2,1)} %bitcast.46, bf16[1536,1024]{1,0:T(8,128)(2,1)S(1)} %bitcast.48), kind=kOutput, calls=%fused_computation.9 | convolution fusion | flops 1207959552 | bytes 5505024 | tf_op jit(solution)/shard_map/dot_general | solution.py:182
  126.9 3.8 %fusion.1 = f32[1152,384]{1,0:T(8,128)} fusion(s32[1152]{0:T(1024)S(1)} %sub.54, bf16[1152,256]{1,0:T(8,128)(2,1)S(1)} %all_to_all.25, bf16[1152,128]{1,0:T(8,128)(2,1)} %copy-done.11), kind=kOutput, calls=%fused_computation.3 | convolution fusion | flops 1022312448 | bytes 2658816 | tf_op jit(solution)/shard_map/dot_general | solution.py:171
  132.6 3.4 %all-to-all-start.3 = ((bf16[8,24,768]{2,1,0:T(8,128)(2,1)}), bf16[8,24,768]{2,1,0:T(8,128)(2,1)S(1)}, u32[]{:S(2)}, u32[]{:S(2)}) async-start(bf16[8,24,768]{2,1,0:T(8,128)(2,1)} %fusion.28), calls=%async_computation.3 | async-start | bytes 589824 | tf_op jit(solution)/shard_map/all_to_all | solution.py:176
  137.9 2.8 %collective-permute-start.23 = (bf16[256,768]{1,0:T(8,128)(2,1)}, bf16[256,768]{1,0:T(8,128)(2,1)}, u32[]{:S(2)}, u32[]{:S(2)}) collective-permute-start(bf16[256,768]{1,0:T(8,128)(2,1)} %fusion.18), channel_id=1, source_target_pairs={{0,128},{128,0},{1,129},{129,1},{2,130},{130,2},{3,131},{131,3},{4... | collective-permute-start | bytes 1179656 | tf_op jit(solution)/shard_map/ppermute | solution.py:36
  142.7 2.9 %fusion.30 = (f32[1,1152,128]{2,1,0:T(8,128)}, f32[1,1152,128]{2,1,0:T(8,128)}, f32[1,1152,128]{2,1,0:T(8,128)}) fusion(f32[1152,128]{1,0:T(8,128)S(1)} %reshape.170, f32[1152,384]{1,0:T(8,128)} %fusion.1), kind=kLoop, calls=%fused_computation.54 | loop fusion | flops 2211840 | bytes 4128768 | tf_op jit(solution)/shard_map/broadcast_in_dim | solution.py:189
  145.6 4.9 %collective-permute-done.23 = bf16[256,768]{1,0:T(8,128)(2,1)} collective-permute-done((bf16[256,768]{1,0:T(8,128)(2,1)}, bf16[256,768]{1,0:T(8,128)(2,1)}, u32[]{:S(2)}, u32[]{:S(2)}) %collective-permute-start.23) | collective-permute-done | bytes 393248 | tf_op jit(solution)/shard_map/ppermute | solution.py:36
  (134 shorter events, 45.7 us)
Async XLA Ops:
  2.4 19.4 %collective-permute-start = (bf16[384,256]{1,0:T(8,128)(2,1)S(1)}, bf16[384,256]{1,0:T(8,128)(2,1)S(1)}, u32[]{:S(2)}, u32[]{:S(2)}) collective-permute-start(bf16[384,256]{1,0:T(8,128)(2,1)S(1)} %slice.125), channel_id=1, source_target_pairs={{0,128},{128,0},{1,129},{129,1},{2,130},{130,2},{3,131},{131,3},{4... | collective-permute-start | bytes 589832 | tf_op jit(solution)/shard_map/ppermute | solution.py:36
  6.1 38.0 %collective-permute-start.11 = (bf16[256,768]{1,0:T(8,128)(2,1)}, bf16[256,768]{1,0:T(8,128)(2,1)}, u32[]{:S(2)}, u32[]{:S(2)}) collective-permute-start(bf16[256,768]{1,0:T(8,128)(2,1)} %refs_10_.1), channel_id=1, source_target_pairs={{0,128},{128,0},{1,129},{129,1},{2,130},{130,2},{3,131},{131,3},{4... | collective-permute-start | bytes 1179656 | tf_op jit(solution)/shard_map/ppermute | solution.py:36
  7.0 27.0 %all-to-all-start = ((bf16[32,36,128]{2,1,0:T(8,128)(2,1)}), bf16[32,36,128]{2,1,0:T(8,128)(2,1)S(1)}, u32[]{:S(2)}, u32[]{:S(2)}) async-start(bf16[32,36,128]{2,1,0:T(8,128)(2,1)} %convert_element_type.130), calls=%async_computation | async-start | bytes 655360 | tf_op jit(solution)/shard_map/all_to_all | solution.py:138
  23.4 17.7 %collective-permute-start.6 = (bf16[192,1024]{1,0:T(8,128)(2,1)S(1)}, bf16[192,1024]{1,0:T(8,128)(2,1)}, u32[]{:S(2)}, u32[]{:S(2)}) collective-permute-start(bf16[192,1024]{1,0:T(8,128)(2,1)S(1)} %pad_maximum_fusion.1.refs_0_), channel_id=1, source_target_pairs={{0,4},{4,0},{1,5},{5,1},{2,6},{6,2},{3,7},{7,3},{8,12},{12,8},{9,1... | collective-permute-start | bytes 1179656 | tf_op jit(solution)/shard_map/ppermute | solution.py:36
  23.9 22.9 %collective-permute-start.2 = (bf16[192,1024]{1,0:T(8,128)(2,1)S(1)}, bf16[192,1024]{1,0:T(8,128)(2,1)S(1)}, u32[]{:S(2)}, u32[]{:S(2)}) collective-permute-start(bf16[192,1024]{1,0:T(8,128)(2,1)S(1)} %pad_maximum_fusion.1.refs_0_), channel_id=1, source_target_pairs={{0,3},{1,0},{2,1},{3,2},{4,7},{5,4},{6,5},{7,6},{8,11},{9,8},{10,9... | collective-permute-start | bytes 1179656 | tf_op jit(solution)/shard_map/ppermute | solution.py:36
  26.6 20.3 %collective-permute-start.4 = (bf16[192,1024]{1,0:T(8,128)(2,1)S(1)}, bf16[192,1024]{1,0:T(8,128)(2,1)S(1)}, u32[]{:S(2)}, u32[]{:S(2)}) collective-permute-start(bf16[192,1024]{1,0:T(8,128)(2,1)S(1)} %pad_maximum_fusion.1.refs_0_), channel_id=1, source_target_pairs={{0,1},{1,2},{2,3},{3,0},{4,5},{5,6},{6,7},{7,4},{8,9},{9,10},{10,1... | collective-permute-start | bytes 1179656 | tf_op jit(solution)/shard_map/ppermute | solution.py:36
  35.8 12.9 %all-to-all-start.1 = ((bf16[8,6,24,128]{3,2,1,0:T(8,128)(2,1)}), bf16[8,6,24,128]{3,2,1,0:T(8,128)(2,1)S(1)}, u32[]{:S(2)}, u32[]{:S(2)}) async-start(bf16[8,6,24,128]{3,2,1,0:T(8,128)(2,1)} %bitcast.2), calls=%async_computation.1 | async-start | bytes 589824 | tf_op jit(solution)/shard_map/all_to_all | solution.py:165
  41.2 14.2 %collective-permute-start.9 = (bf16[192,1024]{1,0:T(8,128)(2,1)}, bf16[192,1024]{1,0:T(8,128)(2,1)}, u32[]{:S(2)}, u32[]{:S(2)}) collective-permute-start(bf16[192,1024]{1,0:T(8,128)(2,1)} %collective-permute-done.6.refs_5_), channel_id=1, source_target_pairs={{0,1},{1,2},{2,3},{3,0},{4,5},{5,6},{6,7},{7,4},{8,9},{9,10},{10,1... | collective-permute-start | bytes 1179656 | tf_op jit(solution)/shard_map/ppermute | solution.py:36
  42.7 12.7 %collective-permute-start.7 = (bf16[192,1024]{1,0:T(8,128)(2,1)}, bf16[192,1024]{1,0:T(8,128)(2,1)}, u32[]{:S(2)}, u32[]{:S(2)}) collective-permute-start(bf16[192,1024]{1,0:T(8,128)(2,1)} %collective-permute-done.6.refs_5_), channel_id=1, source_target_pairs={{0,3},{1,0},{2,1},{3,2},{4,7},{5,4},{6,5},{7,6},{8,11},{9,8},{10,9... | collective-permute-start | bytes 1179656 | tf_op jit(solution)/shard_map/ppermute | solution.py:36
  44.1 16.7 %collective-permute-start.12 = (bf16[256,768]{1,0:T(8,128)(2,1)}, bf16[256,768]{1,0:T(8,128)(2,1)S(1)}, u32[]{:S(2)}, u32[]{:S(2)}) collective-permute-start(bf16[256,768]{1,0:T(8,128)(2,1)} %refs_10_.1), channel_id=1, source_target_pairs={{0,8},{8,0},{1,9},{9,1},{2,10},{10,2},{3,11},{11,3},{4,12},{12,4},... | collective-permute-start | bytes 1179656 | tf_op jit(solution)/shard_map/ppermute | solution.py:36
  46.7 14.1 %collective-permute-start.13 = (bf16[256,768]{1,0:T(8,128)(2,1)}, bf16[256,768]{1,0:T(8,128)(2,1)}, u32[]{:S(2)}, u32[]{:S(2)}) collective-permute-start(bf16[256,768]{1,0:T(8,128)(2,1)} %collective-permute-done.11.refs_11_), channel_id=1, source_target_pairs={{0,8},{8,0},{1,9},{9,1},{2,10},{10,2},{3,11},{11,3},{4,12},{12,4},... | collective-permute-start | bytes 1179656 | tf_op jit(solution)/shard_map/ppermute | solution.py:36
  46.9 14.0 %collective-permute-start.3 = (bf16[96,1024]{1,0:T(8,128)(2,1)S(1)}, bf16[96,1024]{1,0:T(8,128)(2,1)S(1)}, u32[]{:S(2)}, u32[]{:S(2)}) collective-permute-start(bf16[96,1024]{1,0:T(8,128)(2,1)S(1)} %slice.129), channel_id=1, source_target_pairs={{0,3},{1,0},{2,1},{3,2},{4,7},{5,4},{6,5},{7,6},{8,11},{9,8},{10,9... | collective-permute-start | bytes 589832 | tf_op jit(solution)/shard_map/ppermute | solution.py:36
  60.8 16.5 %collective-permute-start.5 = (bf16[96,1024]{1,0:T(8,128)(2,1)}, bf16[96,1024]{1,0:T(8,128)(2,1)}, u32[]{:S(2)}, u32[]{:S(2)}) collective-permute-start(bf16[96,1024]{1,0:T(8,128)(2,1)} %slice.130), channel_id=1, source_target_pairs={{0,1},{1,2},{2,3},{3,0},{4,5},{5,6},{6,7},{7,4},{8,9},{9,10},{10,1... | collective-permute-start | bytes 589832 | tf_op jit(solution)/shard_map/ppermute | solution.py:36
  60.8 16.5 %collective-permute-start.10 = (bf16[96,1024]{1,0:T(8,128)(2,1)}, bf16[96,1024]{1,0:T(8,128)(2,1)}, u32[]{:S(2)}, u32[]{:S(2)}) collective-permute-start(bf16[96,1024]{1,0:T(8,128)(2,1)} %slice.132), channel_id=1, source_target_pairs={{0,1},{1,2},{2,3},{3,0},{4,5},{5,6},{6,7},{7,4},{8,9},{9,10},{10,1... | collective-permute-start | bytes 589832 | tf_op jit(solution)/shard_map/ppermute | solution.py:36
  60.9 16.4 %collective-permute-start.8 = (bf16[96,1024]{1,0:T(8,128)(2,1)}, bf16[96,1024]{1,0:T(8,128)(2,1)}, u32[]{:S(2)}, u32[]{:S(2)}) collective-permute-start(bf16[96,1024]{1,0:T(8,128)(2,1)} %slice.131), channel_id=1, source_target_pairs={{0,3},{1,0},{2,1},{3,2},{4,7},{5,4},{6,5},{7,6},{8,11},{9,8},{10,9... | collective-permute-start | bytes 589832 | tf_op jit(solution)/shard_map/ppermute | solution.py:36
  64.1 25.2 %collective-permute-start.15 = (bf16[8,24,768]{2,1,0:T(8,128)(2,1)}, bf16[8,24,768]{2,1,0:T(8,128)(2,1)}, u32[]{:S(2)}, u32[]{:S(2)}) collective-permute-start(bf16[8,24,768]{2,1,0:T(8,128)(2,1)} %collective-permute-done.14), channel_id=1, source_target_pairs={{0,112},{16,0},{32,16},{48,32},{64,48},{80,64},{96,80},{112,96},{1... | collective-permute-start | bytes 884744 | tf_op jit(solution)/shard_map/ppermute | solution.py:36
  65.4 26.7 %collective-permute-start.18 = (bf16[8,24,768]{2,1,0:T(8,128)(2,1)}, bf16[8,24,768]{2,1,0:T(8,128)(2,1)}, u32[]{:S(2)}, u32[]{:S(2)}) collective-permute-start(bf16[8,24,768]{2,1,0:T(8,128)(2,1)} %collective-permute-done.17), channel_id=1, source_target_pairs={{0,16},{16,32},{32,48},{48,64},{64,80},{80,96},{96,112},{112,0},{1... | collective-permute-start | bytes 884744 | tf_op jit(solution)/shard_map/ppermute | solution.py:36
  67.6 59.1 %all-to-all-start.2 = ((bf16[32,36,256]{2,1,0:T(8,128)(2,1)}), bf16[32,36,256]{2,1,0:T(8,128)(2,1)S(1)}, u32[]{:S(2)}, u32[]{:S(2)}) async-start(bf16[32,36,256]{2,1,0:T(8,128)(2,1)} %all_to_all.23), calls=%async_computation.2 | async-start | bytes 1310720 | tf_op jit(solution)/shard_map/all_to_all | solution.py:169
  89.3 15.1 %collective-permute-start.16 = (bf16[8,24,768]{2,1,0:T(8,128)(2,1)}, bf16[8,24,768]{2,1,0:T(8,128)(2,1)S(1)}, u32[]{:S(2)}, u32[]{:S(2)}) collective-permute-start(bf16[8,24,768]{2,1,0:T(8,128)(2,1)} %collective-permute-done.15), channel_id=1, source_target_pairs={{0,112},{16,0},{32,16},{48,32},{64,48},{80,64},{96,80},{112,96},{1... | collective-permute-start | bytes 884744 | tf_op jit(solution)/shard_map/ppermute | solution.py:36
  92.1 12.1 %collective-permute-start.19 = (bf16[8,24,768]{2,1,0:T(8,128)(2,1)}, bf16[8,24,768]{2,1,0:T(8,128)(2,1)S(1)}, u32[]{:S(2)}, u32[]{:S(2)}) collective-permute-start(bf16[8,24,768]{2,1,0:T(8,128)(2,1)} %collective-permute-done.18), channel_id=1, source_target_pairs={{0,16},{16,32},{32,48},{48,64},{64,80},{80,96},{96,112},{112,0},{1... | collective-permute-start | bytes 884744 | tf_op jit(solution)/shard_map/ppermute | solution.py:36
  96.7 12.6 %collective-permute-start.29 = (bf16[8,24,768]{2,1,0:T(8,128)(2,1)S(1)}, bf16[8,24,768]{2,1,0:T(8,128)(2,1)S(1)}, u32[]{:S(2)}, u32[]{:S(2)}) collective-permute-start(bf16[8,24,768]{2,1,0:T(8,128)(2,1)S(1)} %pad_maximum_fusion.3), channel_id=1, source_target_pairs={{0,112},{16,0},{32,16},{48,32},{64,48},{80,64},{96,80},{112,96},{1... | collective-permute-start | bytes 884744 | tf_op jit(solution)/shard_map/ppermute | solution.py:36
  98.5 12.0 %collective-permute-start.25 = (bf16[8,24,768]{2,1,0:T(8,128)(2,1)S(1)}, bf16[8,24,768]{2,1,0:T(8,128)(2,1)S(1)}, u32[]{:S(2)}, u32[]{:S(2)}) collective-permute-start(bf16[8,24,768]{2,1,0:T(8,128)(2,1)S(1)} %pad_maximum_fusion.2), channel_id=1, source_target_pairs={{0,16},{16,32},{32,48},{48,64},{64,80},{80,96},{96,112},{112,0},{1... | collective-permute-start | bytes 884744 | tf_op jit(solution)/shard_map/ppermute | solution.py:36
  118.1 18.0 %collective-permute-start.22 = (bf16[512,768]{1,0:T(8,128)(2,1)}, bf16[512,768]{1,0:T(8,128)(2,1)}, u32[]{:S(2)}, u32[]{:S(2)}) collective-permute-start(bf16[512,768]{1,0:T(8,128)(2,1)} %fusion.10), channel_id=1, source_target_pairs={{0,8},{8,0},{1,9},{9,1},{2,10},{10,2},{3,11},{11,3},{4,12},{12,4},... | collective-permute-start | bytes 2359304 | tf_op jit(solution)/shard_map/ppermute | solution.py:36
  137.9 12.6 %collective-permute-start.23 = (bf16[256,768]{1,0:T(8,128)(2,1)}, bf16[256,768]{1,0:T(8,128)(2,1)}, u32[]{:S(2)}, u32[]{:S(2)}) collective-permute-start(bf16[256,768]{1,0:T(8,128)(2,1)} %fusion.18), channel_id=1, source_target_pairs={{0,128},{128,0},{1,129},{129,1},{2,130},{130,2},{3,131},{131,3},{4... | collective-permute-start | bytes 1179656 | tf_op jit(solution)/shard_map/ppermute | solution.py:36
  (26 other events, 267.1 us)
